TPU v7x, 512 devices: a whole 4x4x16 slice. The times are simulated.
512 devices in a mesh: row: 16 (over z_hi, y, core), col: 32 (over z_lo, x).
Axes of the slice: x: 4, y: 4, z: 16 (z_hi: 2, z_lo: 8; z = z_hi * 8 + z_lo), core: 2. Of those that a mesh axis runs over, the one named last changes fastest.
Arguments:
- amplitudes: bfloat16 [8192, 4096], P('row', 'col'), may hold values from -6 to 6
- packed_tiles: bfloat16 [16, 512, 128, 128], P('row', 'col'), may hold values from -0.09375 to 0.09375
- tile_ids: int32 [16, 512], P('row', 'col'), may hold values from 0 to 511, as said below
- residual_in: float32 [8192, 32768], P('row', 'col'), may hold values from -6 to 6
Outputs:
- ladder: float32 [8192, 32768], P('row', 'col')
Inputs may be any that keep to these rules, and one draw needn't show every extreme that they name: `tile_ids`: in each grid row the ids are a permutation of 0 to 511; no device holds more than 1 ids of one value of id // 16, and some device holds exactly 1.
All inputs are finite; a program needn't handle non-finite values.
Results may differ from a plain program's by a relative error of at most 0.0003.
Values may be sent and summed in bfloat16 or wider, within the bound.
A program may use at most 64 MiB of HBM per device.

v0:
```python
import jax
import jax.numpy as jnp
from jax import lax
from jax.sharding import PartitionSpec as P

KT_DEV = 2
QT_DEV = 8


def body(amplitudes, packed_tiles, tile_ids, residual_in):
    col_count = lax.axis_size("col")
    col_index = lax.axis_index("col")
    per_device = packed_tiles.shape[1]
    tile_width = packed_tiles.shape[2]
    capacity = (per_device + col_count - 1) // col_count
    slot_total = col_count * capacity
    own_ids = tile_ids[0]
    target_col = own_ids // per_device
    earlier = jnp.arange(per_device)[:, None] > jnp.arange(per_device)[None, :]
    same_target = target_col[:, None] == target_col[None, :]
    order_rank = jnp.sum(earlier & same_target, axis=1)
    slot_of = target_col * capacity + order_rank
    chooser = (jnp.arange(slot_total)[:, None] == slot_of[None, :]).astype(jnp.float32)
    outgoing = jnp.einsum(
        "sl,lij->sij",
        chooser.astype(jnp.bfloat16),
        packed_tiles[0],
        preferred_element_type=jnp.float32,
    )
    outgoing = outgoing.astype(jnp.bfloat16).reshape(col_count, capacity, tile_width, tile_width)
    all_ids = lax.all_gather(tile_ids, "col", axis=1, tiled=True)[0]
    incoming = lax.all_to_all(outgoing, "col", split_axis=0, concat_axis=0, tiled=True)
    source_ids = all_ids.reshape(col_count, per_device)
    source_target = source_ids // per_device
    source_same = source_target[:, :, None] == source_target[:, None, :]
    source_rank = jnp.sum(source_same & earlier[None], axis=2)
    source_slot = (jnp.arange(col_count)[:, None] * capacity + source_rank).reshape(-1)
    for_me = (source_target == col_index).reshape(-1)
    source_pos = (source_ids % per_device).reshape(-1)
    pos_table = ((jnp.arange(per_device)[:, None] == source_pos[None, :]) & for_me[None, :]).astype(
        jnp.float32
    )
    slot_table = (jnp.arange(slot_total)[:, None] == source_slot[None, :]).astype(jnp.float32)
    unpack = jnp.dot(pos_table, slot_table.T)
    unpacked = jnp.einsum(
        "ps,sij->pij",
        unpack.astype(jnp.bfloat16),
        incoming.reshape(slot_total, tile_width, tile_width),
        preferred_element_type=jnp.float32,
    )
    unpacked = unpacked.astype(jnp.bfloat16).reshape(KT_DEV, QT_DEV, tile_width, tile_width)
    integral_block = unpacked.transpose(0, 2, 1, 3).reshape(
        KT_DEV * tile_width, QT_DEV * tile_width
    )
    amp_full = lax.all_gather(amplitudes, "col", axis=1, tiled=True)
    product = jnp.dot(
        amp_full,
        lax.all_gather(integral_block, "row", axis=0, tiled=True),
        preferred_element_type=jnp.float32,
    )
    return residual_in + product


def solution(mesh):
    in_specs = (P("row", "col"), P("row", "col", None, None), P("row", "col"), P("row", "col"))
    out_specs = P("row", "col")
    return jax.shard_map(body, mesh=mesh, in_specs=in_specs, out_specs=out_specs, check_vma=False)
```

profile of v0, /device:TPU:1, one launch (start us, length us, event | category | flops | bytes accessed | tf_op | source)
XLA Modules:
  0.0 408.5 jit_solution(14928709801954503088)
XLA Ops:
  6.5 0.0 copy-start
  6.5 0.0 all-gather.5.cloned.1.call-start
  6.5 0.7 all-gather.5.cloned.1.call-update
  7.3 1.3 dynamic-slice
  9.2 0.7 fusion.23
  9.9 0.7 bitcast_dynamic-update-slice_fusion
  10.6 0.2 convert_reduce_fusion.1
  10.8 0.7 fusion.20
  11.5 0.0 copy-done
  11.5 0.6 fusion
  12.1 1.4 copy.22
  13.4 15.9 %all-to-all-start = ((bf16[32,1,128,128]{3,2,1,0:T(8,128)(2,1)}), bf16[32,1,128,128]{3,2,1,0:T(8,128)(2,1)S(1)}, u32[]{:S(2)}, u32[]{:S(2)}) async-start(bf16[32,1,128,128]{3,2,1,0:T(8,128)(2,1)} %copy.22), calls=%async_computation | async-start | bytes 2097152 | tf_op jit(solution)/shard_map/all_to_all | solution.py:32
  29.4 0.0 all-gather.3.cloned.1.call-start
  29.4 58.7 %all-reduce = s32[512]{0:T(512)S(1)} all-reduce(s32[512]{0:T(512)S(1)} %get-tuple-element.7), channel_id=1, replica_groups=mesh['row'=16,'col'=32] {'col'}, use_global_device_ids=true, to_apply=%add | all-reduce | flops 512 | bytes 4096
  88.2 0.1 reshape_squeeze.3
  88.3 0.1 copy.18
  88.3 0.1 convert_reduce_fusion
  88.5 0.1 copy.20
  88.5 0.1 add.51
  88.7 0.0 all-to-all-done
  88.7 0.7 fusion.1
  89.5 0.9 copy.35
  90.4 0.0 all-gather.3.cloned.1.call-update
  90.4 1.9 copy.25
  92.3 105.3 %all-gather.5.cloned.1.call-done = bf16[512,4096]{1,0:T(8,128)(2,1)} async-done(((bf16[512,128]{1,0:T(8,128)(2,1)}), bf16[512,4096]{1,0:T(8,128)(2,1)}) %all-gather.5.cloned.1.call-update) | async-done | bytes 4194320 | tf_op jit(solution)/shard_map/all_gather | solution.py:55
  197.6 190.7 %all-gather.3.cloned.1.call-done = bf16[4096,1024]{1,0:T(8,128)(2,1)} async-done(((bf16[256,1024]{1,0:T(8,128)(2,1)}), bf16[4096,1024]{1,0:T(8,128)(2,1)}) %all-gather.3.cloned.1.call-update) | async-done | bytes 8388624 | tf_op jit(solution)/shard_map/all_gather | solution.py:58
  388.3 10.5 %bitcast_add_fusion = f32[512,1024]{0,1:T(8,128)} fusion(f32[512,1024]{0,1:T(8,128)S(1)} %copy.25, bf16[4096,1024]{1,0:T(8,128)(2,1)} %all-gather.3.cloned.1.call-done, bf16[512,4096]{1,0:T(8,128)(2,1)} %all-gather.5.cloned.1.call-done), kind=kOutput, calls=%fused_computation | convolution fusion | flops 4295491584 | bytes 16777216 | tf_op jit(solution)/shard_map/dot_general | solution.py:56
  398.8 2.9 copy.26
  (7 shorter events, 0.1 us)
Async XLA Ops:
  6.5 4.9 %copy-start = (bf16[1,16,128,128]{3,2,1,0:T(8,128)(2,1)S(1)}, bf16[1,16,128,128]{3,2,1,0:T(8,128)(2,1)}, u32[]{:S(2)}) copy-start(bf16[1,16,128,128]{3,2,1,0:T(8,128)(2,1)} %param.5) | copy-start | bytes 1572868
  6.5 191.1 %all-gather.5.cloned.1.call-start = ((), (), s32[]{:S(2)}) async-start(), calls=%async_computation.2 | async-start | bytes 4325376 | tf_op jit(solution)/shard_map/all_gather | solution.py:55
  13.4 75.2 %all-to-all-start = ((bf16[32,1,128,128]{3,2,1,0:T(8,128)(2,1)}), bf16[32,1,128,128]{3,2,1,0:T(8,128)(2,1)S(1)}, u32[]{:S(2)}, u32[]{:S(2)}) async-start(bf16[32,1,128,128]{3,2,1,0:T(8,128)(2,1)} %copy.22), calls=%async_computation | async-start | bytes 2097152 | tf_op jit(solution)/shard_map/all_to_all | solution.py:32
  29.4 359.0 %all-gather.3.cloned.1.call-start = ((), (), s32[]{:S(2)}) async-start(), calls=%async_computation.1 | async-start | bytes 8912896 | tf_op jit(solution)/shard_map/all_gather | solution.py:58
Sparse Core Ops, SparseCore 0:
  9.4 188.2 all-gather.4
  200.9 187.3 all-gather.2
where the time goes:
time: 409 us
  waiting for transfers between devices  297 us (73%)
  blocking collectives  58.7 us (14%)
  starting transfers between devices  16 us (4%)
  between operations  14.1 us (3%)
  matrix products  11.8 us (3%)
  local copies, waits for them, and re-layouts  8.69 us (2%)
    all_gather x1, waiting for transfers between devices, body(): lax.all_gather(integral_block, 'row', axis=0, tiled=True)  191 us
    all_gather x1, waiting for transfers between devices, body(): amp_full = lax.all_gather(amplitudes, 'col', axis=1, tiled=True)  105 us
    unnamed x1, blocking collectives  58.7 us
    all_to_all x1, starting transfers between devices, body(): lax.all_to_all(outgoing, 'col', split_axis=0, concat_axis=0, tiled=True)  15.9 us
    dot_general x1, matrix products, body(): jnp.dot(amp_full, lax.all_gather(integral_block, 'row', axis=0, tiled=Tru...  10.5 us
  transfers between devices with their start and end apart: 3, of which 2 were waited for; matrix products, arithmetic and copies ran while one was open for 2% of the time, Pallas kernels for 0%

commit v1 on v0

v1 whole, which is shorter than its diff:
```python
import jax
import jax.numpy as jnp
from jax import lax
from jax.sharding import Mesh
from jax.sharding import PartitionSpec as P

ROW_AXES = ("z_hi", "y", "core")
COL_AXES = ("z_lo", "x")
ROW_SPLIT = (2, 4, 2)
COL_SPLIT = (8, 4)


def body(amplitudes, packed_tiles, tile_ids, residual_in):
    per_device = packed_tiles.shape[1]
    tile = packed_tiles.shape[2]
    col_count = COL_SPLIT[0] * COL_SPLIT[1]
    own_ids = tile_ids[0]
    target_col = own_ids // per_device
    position = own_ids % per_device
    chooser = (jnp.arange(col_count)[:, None] == target_col[None, :]).astype(jnp.bfloat16)
    tag_rows = jnp.broadcast_to(
        (position + 1).astype(jnp.bfloat16)[:, None, None], (per_device, 16, tile)
    )
    tagged = jnp.concatenate([packed_tiles[0], tag_rows], axis=1)
    outgoing = jnp.einsum("sl,lij->sij", chooser, tagged, preferred_element_type=jnp.float32)
    outgoing = outgoing.astype(jnp.bfloat16)
    incoming = lax.all_to_all(outgoing, COL_AXES, split_axis=0, concat_axis=0, tiled=True)
    tags = incoming[:, tile, 0].astype(jnp.float32)
    unpack = (
        (jnp.arange(per_device, dtype=jnp.float32)[:, None] + 1.0) == tags[None, :]
    ).astype(jnp.bfloat16)
    unpacked = jnp.einsum(
        "ps,sij->pij", unpack, incoming[:, :tile, :], preferred_element_type=jnp.float32
    ).astype(jnp.bfloat16)
    kt = 2
    qt = per_device // kt
    block = unpacked.reshape(kt, qt, tile, tile).transpose(0, 2, 1, 3).reshape(kt, tile, qt * tile)
    g = lax.all_gather(block, "z_hi")
    g = lax.all_gather(g, "y")
    g = lax.all_gather(g, "core")
    a = lax.all_gather(amplitudes, "z_lo")
    a = lax.all_gather(a, "x")
    a = a.reshape(2, 2, 2, 4, a.shape[2], a.shape[3])
    product = jnp.einsum("ckhypj,cyhkjn->pn", a, g, preferred_element_type=jnp.float32)
    return residual_in + product


def solution(mesh):
    devices = mesh.devices.reshape(ROW_SPLIT + COL_SPLIT)
    fine = Mesh(devices, ROW_AXES + COL_AXES)
    row, col = ROW_AXES, COL_AXES
    in_specs = (P(row, col), P(row, col, None, None), P(row, col), P(row, col))
    out_specs = P(row, col)
    return jax.shard_map(body, mesh=fine, in_specs=in_specs, out_specs=out_specs, check_vma=False)
```

time: 409 us -> 382 us (0.934)
  blocking collectives: 58.7 us -> 0 us
  waiting for transfers between devices: 297 us -> 331 us
    unnamed x1 -> x0, blocking collectives: 58.7 us -> none
    all_to_all x1, waiting for transfers between devices: 0.01 us -> 55.2 us  [body(): lax.all_to_all(outgoing, COL_AXES, split_axis=0, concat_axis=0, tiled=True)]
    all_gather x2 -> x5, waiting for transfers between devices: 296 us -> 275 us  [the longest x1 72.4 us: body(): g = lax.all_gather(block, 'z_hi')]
  transfers between devices with their start and end apart: 3 -> 6, of which waited for: 2 -> 6; matrix products, arithmetic and copies ran while one was open for 2% -> 0% of each run, Pallas kernels for 0% -> 0%
where the time goes in v1:
time: 382 us
  waiting for transfers between devices  331 us (87%)
  starting transfers between devices  16.1 us (4%)
  between operations  13.2 us (3%)
  matrix products  11.1 us (3%)
  local copies, waits for them, and re-layouts  9.28 us (2%)
    all_gather x1, waiting for transfers between devices, body(): g = lax.all_gather(block, 'z_hi')  72.4 us
    all_gather x1, waiting for transfers between devices, body(): g = lax.all_gather(g, 'y')  57.9 us
    all_gather x1, waiting for transfers between devices, body(): a = lax.all_gather(amplitudes, 'z_lo')  55.3 us
    all_to_all x1, waiting for transfers between devices, body(): lax.all_to_all(outgoing, COL_AXES, split_axis=0, concat_axis=0, tiled=True)  55.2 us
    all_gather x1, waiting for transfers between devices, body(): a = lax.all_gather(a, 'x')  54.9 us
    all_gather x1, waiting for transfers between devices, body(): g = lax.all_gather(g, 'core')  34.2 us
    all_to_all x1, starting transfers between devices, body(): lax.all_to_all(outgoing, COL_AXES, split_axis=0, concat_axis=0, tiled=True)  15.9 us
    dot_general x1, matrix products, body(): jnp.einsum('ckhypj,cyhkjn->pn', a, g, preferred_element_type=jnp.float32)  9.79 us
  transfers between devices with their start and end apart: 6, of which 6 were waited for; matrix products, arithmetic and copies ran while one was open for 0% of the time, Pallas kernels for 0%

profile of v1, /device:TPU:1, one launch (start us, length us, event | category | flops | bytes accessed | tf_op | source)
XLA Modules:
  0.0 382.0 jit_solution(6040744895554465881)
XLA Ops:
  6.5 0.7 fusion.21
  7.2 0.7 fusion.23
  7.9 1.4 copy.38
  9.2 0.1 broadcast_in_dim.2
  9.3 0.6 convolution_convert_fusion
  9.9 1.5 copy.15
  11.4 15.9 %all-to-all-start = ((bf16[32,144,128]{2,1,0:T(8,128)(2,1)}), bf16[32,144,128]{2,1,0:T(8,128)(2,1)S(1)}, u32[]{:S(2)}, u32[]{:S(2)}) async-start(bf16[32,144,128]{2,1,0:T(8,128)(2,1)} %copy.15), calls=%async_computation | async-start | bytes 2359296 | tf_op jit(solution)/shard_map/all_to_all | solution.py:27
  27.3 0.0 all-gather.10.cloned.1.call-start
  27.4 55.2 %all-to-all-done = bf16[32,144,128]{2,1,0:T(8,128)(2,1)S(1)} async-done(((bf16[32,144,128]{2,1,0:T(8,128)(2,1)}), bf16[32,144,128]{2,1,0:T(8,128)(2,1)S(1)}, u32[]{:S(2)}, u32[]{:S(2)}) %all-to-all-start) | async-done | bytes 1179680 | tf_op jit(solution)/shard_map/all_to_all | solution.py:27
  82.6 0.1 slice.9
  82.7 0.3 fusion.12
  83.0 0.7 fusion.7
  83.7 0.1 reshape.52
  83.9 0.9 copy.24
  84.8 0.0 all-gather.10.cloned.1.call-update
  84.8 0.0 all-gather.16.cloned.1.call-start
  84.9 0.7 all-gather.16.cloned.1.call-update
  85.6 0.0 all-gather.12.cloned.1.call-start
  85.6 72.4 %all-gather.10.cloned.1.call-done = bf16[2,2,128,1024]{3,2,1,0:T(8,128)(2,1)} async-done(((bf16[1,2,128,1024]{3,2,1,0:T(8,128)(2,1)}), bf16[2,2,128,1024]{3,2,1,0:T(8,128)(2,1)}) %all-gather.10.cloned.1.call-update) | async-done | bytes 1048592 | tf_op jit(solution)/shard_map/all_gather | solution.py:38
  158.1 0.0 all-gather.12.cloned.1.call-update
  158.1 0.0 all-gather.18.cloned.1.call-start
  158.1 55.3 %all-gather.16.cloned.1.call-done = bf16[4096,128]{1,0:T(8,128)(2,1)} async-done(((bf16[512,128]{1,0:T(8,128)(2,1)}), bf16[4096,128]{1,0:T(8,128)(2,1)}) %all-gather.16.cloned.1.call-update) | async-done | bytes 1048592 | tf_op jit(solution)/shard_map/all_gather | solution.py:41
  213.4 0.0 all-gather.18.cloned.1.call-update
  213.5 0.0 all-gather.14.cloned.1.call-start
  213.5 57.9 %all-gather.12.cloned.1.call-done = bf16[8,2,128,1024]{3,2,1,0:T(8,128)(2,1)} async-done(((bf16[2,2,128,1024]{3,2,1,0:T(8,128)(2,1)}), bf16[8,2,128,1024]{3,2,1,0:T(8,128)(2,1)}) %all-gather.12.cloned.1.call-update) | async-done | bytes 4194320 | tf_op jit(solution)/shard_map/all_gather | solution.py:39
  271.4 0.0 copy-start
  271.4 0.0 all-gather.14.cloned.1.call-update
  271.4 1.6 copy-done
  273.0 1.8 copy.20
  274.8 54.9 %all-gather.18.cloned.1.call-done = bf16[32,512,128]{2,1,0:T(8,128)(2,1)} async-done(((bf16[8,512,128]{2,1,0:T(8,128)(2,1)}), bf16[32,512,128]{2,1,0:T(8,128)(2,1)}) %all-gather.18.cloned.1.call-update) | async-done | bytes 4194320 | tf_op jit(solution)/shard_map/all_gather | solution.py:42
  329.7 34.2 %all-gather.14.cloned.1.call-done = bf16[8,2,2,128,1024]{4,3,2,1,0:T(8,128)(2,1)} async-done(((bf16[4,2,2,128,1024]{4,3,2,1,0:T(8,128)(2,1)}), bf16[8,2,2,128,1024]{4,3,2,1,0:T(8,128)(2,1)}) %all-gather.14.cloned.1.call-update) | async-done | bytes 8388624 | tf_op jit(solution)/shard_map/all_gather | solution.py:40
  363.9 9.8 %bitcast_add_fusion = f32[512,1024]{0,1:T(8,128)S(1)} fusion(f32[512,1024]{0,1:T(8,128)} %copy.20, bf16[2,2,2,4,512,128]{5,4,3,2,1,0:T(8,128)(2,1)} %bitcast.35, bf16[2,4,2,2,128,1024]{5,4,3,2,1,0:T(8,128)(2,1)} %bitcast.34), kind=kOutput, calls=%fused_computation.3 | convolution fusion | flops 4295491584 | bytes 16777216 | tf_op jit(solution)/shard_map/ckhypj,cyhkjn->pn/dot_general | solution.py:44
  373.7 1.8 copy.21
  (1 shorter events, 0.0 us)
Async XLA Ops:
  11.4 71.2 %all-to-all-start = ((bf16[32,144,128]{2,1,0:T(8,128)(2,1)}), bf16[32,144,128]{2,1,0:T(8,128)(2,1)S(1)}, u32[]{:S(2)}, u32[]{:S(2)}) async-start(bf16[32,144,128]{2,1,0:T(8,128)(2,1)} %copy.15), calls=%async_computation | async-start | bytes 2359296 | tf_op jit(solution)/shard_map/all_to_all | solution.py:27
  27.3 130.7 %all-gather.10.cloned.1.call-start = ((), (), s32[]{:S(2)}) async-start(), calls=%async_computation.1 | async-start | bytes 1572864 | tf_op jit(solution)/shard_map/all_gather | solution.py:38
  84.8 128.6 %all-gather.16.cloned.1.call-start = ((), (), s32[]{:S(2)}) async-start(), calls=%async_computation.4 | async-start | bytes 1179648 | tf_op jit(solution)/shard_map/all_gather | solution.py:41
  85.6 185.8 %all-gather.12.cloned.1.call-start = ((), (), s32[]{:S(2)}) async-start(), calls=%async_computation.2 | async-start | bytes 5242880 | tf_op jit(solution)/shard_map/all_gather | solution.py:39
  158.1 171.6 %all-gather.18.cloned.1.call-start = ((), (), s32[]{:S(2)}) async-start(), calls=%async_computation.5 | async-start | bytes 5242880 | tf_op jit(solution)/shard_map/all_gather | solution.py:42
  213.5 150.4 %all-gather.14.cloned.1.call-start = ((), (), s32[]{:S(2)}) async-start(), calls=%async_computation.3 | async-start | bytes 12582912 | tf_op jit(solution)/shard_map/all_gather | solution.py:40
  271.4 1.6 copy-start
Sparse Core Ops, SparseCore 0:
  84.9 73.0 all-gather.9
  160.1 53.2 all-gather.15
  215.5 55.8 all-gather.11
  273.4 56.2 all-gather.17
  331.6 32.1 all-gather.13

commit v2 on v1

--- a/solution.py
+++ b/solution.py
@@ -1,6 +1,10 @@
+import functools
+
 import jax
 import jax.numpy as jnp
 from jax import lax
+from jax.experimental import pallas as pl
+from jax.experimental.pallas import tpu as pltpu
 from jax.sharding import Mesh
 from jax.sharding import PartitionSpec as P
 
@@ -8,6 +12,52 @@
 COL_AXES = ("z_lo", "x")
 ROW_SPLIT = (2, 4, 2)
 COL_SPLIT = (8, 4)
+MESH = pl.DeviceIdType.MESH
+
+
+def gather_kernel(axis, n, x_ref, o_ref, send_sem, recv_sem, local_sem):
+    me = lax.axis_index(axis)
+    barrier = pltpu.get_barrier_semaphore()
+    for j in range(1, n):
+        peer = lax.rem(me + j, n)
+        pl.semaphore_signal(barrier, inc=1, device_id={axis: peer}, device_id_type=MESH)
+    pl.semaphore_wait(barrier, n - 1)
+    local = pltpu.make_async_copy(x_ref, o_ref.at[me], local_sem)
+    local.start()
+    copies = []
+    for j in range(1, n):
+        peer = lax.rem(me + j, n)
+        copy = pltpu.make_async_remote_copy(
+            src_ref=x_ref,
+            dst_ref=o_ref.at[me],
+            send_sem=send_sem.at[j],
+            recv_sem=recv_sem.at[j],
+            device_id={axis: peer},
+            device_id_type=MESH,
+        )
+        copy.start()
+        copies.append(copy)
+    local.wait()
+    for copy in copies:
+        copy.wait()
+
+
+def gather(x, axis, n, cid):
+    nbytes = x.size * x.dtype.itemsize
+    return pl.pallas_call(
+        functools.partial(gather_kernel, axis, n),
+        out_shape=jax.ShapeDtypeStruct((n,) + x.shape, x.dtype),
+        in_specs=[pl.BlockSpec(memory_space=pl.ANY)],
+        out_specs=pl.BlockSpec(memory_space=pl.ANY),
+        scratch_shapes=[
+            pltpu.SemaphoreType.DMA((n,)),
+            pltpu.SemaphoreType.DMA((n,)),
+            pltpu.SemaphoreType.DMA(()),
+        ],
+        compiler_params=pltpu.CompilerParams(collective_id=cid, has_side_effects=True),
+        cost_estimate=pl.CostEstimate(flops=0, transcendentals=0, bytes_accessed=2 * n * nbytes),
+        name=f"gather_{axis}",
+    )(x)
 
 
 def body(amplitudes, packed_tiles, tile_ids, residual_in):
@@ -35,11 +85,11 @@
     kt = 2
     qt = per_device // kt
     block = unpacked.reshape(kt, qt, tile, tile).transpose(0, 2, 1, 3).reshape(kt, tile, qt * tile)
-    g = lax.all_gather(block, "z_hi")
-    g = lax.all_gather(g, "y")
-    g = lax.all_gather(g, "core")
-    a = lax.all_gather(amplitudes, "z_lo")
-    a = lax.all_gather(a, "x")
+    g = gather(block, "z_hi", ROW_SPLIT[0], 0)
+    g = gather(g, "y", ROW_SPLIT[1], 1)
+    g = gather(g, "core", ROW_SPLIT[2], 2)
+    a = gather(amplitudes, "z_lo", COL_SPLIT[0], 3)
+    a = gather(a, "x", COL_SPLIT[1], 4)
     a = a.reshape(2, 2, 2, 4, a.shape[2], a.shape[3])
     product = jnp.einsum("ckhypj,cyhkjn->pn", a, g, preferred_element_type=jnp.float32)
     return residual_in + product

time: 382 us -> 416 us (1.089)
  the two profiles are of different devices: /device:TPU:1 before, /device:TPU:227 now
where the time goes in v2:
time: 416 us; the launch traced here: 415 us
  Pallas kernels  381 us (92%)
  starting transfers between devices  12 us (3%)
  matrix products  11.7 us (3%)
  local copies, waits for them, and re-layouts  8.82 us (2%)
    pallas_call x5, Pallas kernels, gather(): pl.pallas_call(functools.partial(gather_kernel, axis, n), out_shape=jax.S...  381 us
    all_to_all x1, starting transfers between devices, body(): lax.all_to_all(outgoing, COL_AXES, split_axis=0, concat_axis=0, tiled=True)  12 us
    dot_general x1, matrix products, body(): jnp.einsum('ckhypj,cyhkjn->pn', a, g, preferred_element_type=jnp.float32)  10.5 us
  transfers between devices with their start and end apart: 1, of which 0 were waited for; matrix products, arithmetic and copies ran while one was open for 0% of the time, Pallas kernels for 35%

profile of v2, /device:TPU:227, one launch (start us, length us, event | category | flops | bytes accessed | tf_op | source)
XLA Modules:
  0.0 415.2 jit_solution(13844785270961505048)
XLA Ops:
  0.0 0.7 fusion.21
  0.7 0.7 fusion.23
  1.3 1.4 copy.42
  2.7 0.1 broadcast_in_dim.2
  2.8 0.6 convolution_convert_fusion
  3.4 1.5 copy.18
  4.8 12.0 %all-to-all-start = ((bf16[32,144,128]{2,1,0:T(8,128)(2,1)}), bf16[32,144,128]{2,1,0:T(8,128)(2,1)S(1)}, u32[]{:S(2)}, u32[]{:S(2)}) async-start(bf16[32,144,128]{2,1,0:T(8,128)(2,1)} %copy.18), calls=%async_computation | async-start | bytes 2359296 | tf_op jit(solution)/shard_map/all_to_all | solution.py:77
  16.9 96.9 %gather_z_lo.1.x_ref = bf16[8,512,128]{2,1,0:T(8,128)(2,1)} custom-call(bf16[512,128]{1,0:T(8,128)(2,1)} %x_ref.1), custom_call_target="tpu_custom_call" | custom-call | bytes 2097152 | tf_op jit(solution)/shard_map/gather_z_lo/pallas_call | solution.py:47
  113.7 0.0 copy-start
  113.7 48.7 %gather_x.1 = bf16[4,8,512,128]{3,2,1,0:T(8,128)(2,1)} custom-call(bf16[8,512,128]{2,1,0:T(8,128)(2,1)} %gather_z_lo.1.x_ref), custom_call_target="tpu_custom_call" | custom-call | bytes 8388608 | tf_op jit(solution)/shard_map/gather_x/pallas_call | solution.py:47
  162.5 0.0 copy-done
  162.5 1.8 copy.23
  164.3 0.0 all-to-all-done
  164.3 0.1 slice.9
  164.4 0.3 fusion.12
  164.7 0.7 fusion.7
  165.5 1.0 reshape.45.x_ref
  166.5 54.6 %gather_z_hi.1.x_ref = bf16[2,2,128,1024]{3,2,1,0:T(8,128)(2,1)} custom-call(bf16[2,128,1024]{2,1,0:T(8,128)(2,1)} %reshape.45.x_ref), custom_call_target="tpu_custom_call" | custom-call | bytes 2097152 | tf_op jit(solution)/shard_map/gather_z_hi/pallas_call | solution.py:47
  221.2 50.3 %gather_y.1.x_ref = bf16[4,2,2,128,1024]{4,3,2,1,0:T(8,128)(2,1)} custom-call(bf16[2,2,128,1024]{3,2,1,0:T(8,128)(2,1)} %gather_z_hi.1.x_ref), custom_call_target="tpu_custom_call" | custom-call | bytes 8388608 | tf_op jit(solution)/shard_map/gather_y/pallas_call | solution.py:47
  271.5 0.0 copy-start.1
  271.5 130.4 %gather_core.1 = bf16[2,4,2,2,128,1024]{5,4,3,2,1,0:T(8,128)(2,1)} custom-call(bf16[4,2,2,128,1024]{4,3,2,1,0:T(8,128)(2,1)} %gather_y.1.x_ref), custom_call_target="tpu_custom_call" | custom-call | bytes 16777216 | tf_op jit(solution)/shard_map/gather_core/pallas_call | solution.py:47
  401.9 0.0 copy-done.1
  401.9 10.5 %bitcast_add_fusion = f32[512,1024]{0,1:T(8,128)} fusion(f32[512,1024]{0,1:T(8,128)S(1)} %copy-done.1, bf16[2,2,2,4,512,128]{5,4,3,2,1,0:T(8,128)(2,1)} %bitcast.27, bf16[2,4,2,2,128,1024]{5,4,3,2,1,0:T(8,128)(2,1)} %gather_core.1), kind=kOutput, calls=%fused_computation.3 | convolution fusion | flops 4295491584 | bytes 16777216 | tf_op jit(solution)/shard_map/ckhypj,cyhkjn->pn/dot_general | solution.py:94
  412.3 2.9 copy.24
  (2 shorter events, 0.0 us)
Async XLA Ops:
  4.8 159.5 %all-to-all-start = ((bf16[32,144,128]{2,1,0:T(8,128)(2,1)}), bf16[32,144,128]{2,1,0:T(8,128)(2,1)S(1)}, u32[]{:S(2)}, u32[]{:S(2)}) async-start(bf16[32,144,128]{2,1,0:T(8,128)(2,1)} %copy.18), calls=%async_computation | async-start | bytes 2359296 | tf_op jit(solution)/shard_map/all_to_all | solution.py:77
  113.7 48.7 %copy-start = (f32[512,1024]{1,0:T(8,128)S(1)}, f32[512,1024]{1,0:T(8,128)}, u32[]{:S(2)}) copy-start(f32[512,1024]{1,0:T(8,128)} %param.7) | copy-start | bytes 6291460
  271.5 130.4 %copy-start.1 = (f32[512,1024]{0,1:T(8,128)S(1)}, f32[512,1024]{0,1:T(8,128)}, u32[]{:S(2)}) copy-start(f32[512,1024]{0,1:T(8,128)} %copy.23) | copy-start | bytes 6291460

commit v3 on v2

--- a/solution.py
+++ b/solution.py
@@ -15,15 +15,13 @@
 MESH = pl.DeviceIdType.MESH
 
 
-def gather_kernel(axis, n, x_ref, o_ref, send_sem, recv_sem, local_sem):
+def gather_kernel(axis, n, x_ref, o_ref, send_sem, recv_sem):
     me = lax.axis_index(axis)
     barrier = pltpu.get_barrier_semaphore()
     for j in range(1, n):
         peer = lax.rem(me + j, n)
         pl.semaphore_signal(barrier, inc=1, device_id={axis: peer}, device_id_type=MESH)
     pl.semaphore_wait(barrier, n - 1)
-    local = pltpu.make_async_copy(x_ref, o_ref.at[me], local_sem)
-    local.start()
     copies = []
     for j in range(1, n):
         peer = lax.rem(me + j, n)
@@ -37,14 +35,13 @@
         )
         copy.start()
         copies.append(copy)
-    local.wait()
     for copy in copies:
         copy.wait()
 
 
 def gather(x, axis, n, cid):
     nbytes = x.size * x.dtype.itemsize
-    return pl.pallas_call(
+    out = pl.pallas_call(
         functools.partial(gather_kernel, axis, n),
         out_shape=jax.ShapeDtypeStruct((n,) + x.shape, x.dtype),
         in_specs=[pl.BlockSpec(memory_space=pl.ANY)],
@@ -52,12 +49,12 @@
         scratch_shapes=[
             pltpu.SemaphoreType.DMA((n,)),
             pltpu.SemaphoreType.DMA((n,)),
-            pltpu.SemaphoreType.DMA(()),
         ],
         compiler_params=pltpu.CompilerParams(collective_id=cid, has_side_effects=True),
         cost_estimate=pl.CostEstimate(flops=0, transcendentals=0, bytes_accessed=2 * n * nbytes),
         name=f"gather_{axis}",
     )(x)
+    return lax.dynamic_update_slice_in_dim(out, x[None], lax.axis_index(axis), axis=0)
 
 
 def body(amplitudes, packed_tiles, tile_ids, residual_in):

time: 416 us -> 296 us (0.71)
  Pallas kernels: 381 us -> 260 us
  local copies, waits for them, and re-layouts: 8.82 us -> 13 us
    pallas_call x5, Pallas kernels: 381 us -> 260 us  [gather(): pl.pallas_call(functools.partial(gather_kernel, axis, n), out_shape=jax.S...]
    dynamic_update_slice x0 -> x5, local copies, waits for them, and re-layouts: none -> 8.59 us  [gather(): lax.dynamic_update_slice_in_dim(out, x[None], lax.axis_index(axis), axis=0)]
  transfers between devices with their start and end apart: 1 -> 1, of which waited for: 0 -> 0; matrix products, arithmetic and copies ran while one was open for 0% -> 1% of each run, Pallas kernels for 35% -> 49%
where the time goes in v3:
time: 296 us
  Pallas kernels  260 us (88%)
  local copies, waits for them, and re-layouts  13 us (4%)
  starting transfers between devices  12 us (4%)
  matrix products  9.09 us (3%)
    pallas_call x5, Pallas kernels, gather(): pl.pallas_call(functools.partial(gather_kernel, axis, n), out_shape=jax.S...  260 us
    all_to_all x1, starting transfers between devices, body(): lax.all_to_all(outgoing, COL_AXES, split_axis=0, concat_axis=0, tiled=True)  12 us
    dynamic_update_slice x5, local copies, waits for them, and re-layouts, gather(): lax.dynamic_update_slice_in_dim(out, x[None], lax.axis_index(axis), axis=0)  8.59 us
    dot_general x1, matrix products, body(): jnp.einsum('ckhypj,cyhkjn->pn', a, g, preferred_element_type=jnp.float32)  7.83 us
  transfers between devices with their start and end apart: 1, of which 0 were waited for; matrix products, arithmetic and copies ran while one was open for 1% of the time, Pallas kernels for 49%

profile of v3, /device:TPU:227, one launch (start us, length us, event | category | flops | bytes accessed | tf_op | source)
XLA Modules:
  0.0 295.7 jit_solution(6013452448928309469)
XLA Ops:
  0.0 0.7 fusion.21
  0.7 0.7 fusion.23
  1.3 0.0 copy-start.3
  1.3 1.4 copy.34
  2.8 0.1 broadcast_in_dim.24
  2.8 0.6 convolution_convert_fusion
  3.4 1.5 copy.14
  4.9 12.0 %all-to-all-start = ((bf16[32,144,128]{2,1,0:T(8,128)(2,1)}), bf16[32,144,128]{2,1,0:T(8,128)(2,1)S(1)}, u32[]{:S(2)}, u32[]{:S(2)}) async-start(bf16[32,144,128]{2,1,0:T(8,128)(2,1)} %copy.14), calls=%async_computation | async-start | bytes 2359296 | tf_op jit(solution)/shard_map/all_to_all | solution.py:74
  16.9 96.8 %gather_z_lo.1 = bf16[8,512,128]{2,1,0:T(8,128)(2,1)} custom-call(bf16[512,128]{1,0:T(8,128)(2,1)} %x_ref.1), custom_call_target="tpu_custom_call" | custom-call | bytes 2097152 | tf_op jit(solution)/shard_map/gather_z_lo/pallas_call | solution.py:44
  113.8 0.0 copy-done.3
  113.8 0.7 bitcast_dynamic-update-slice_fusion.3.x_ref
  114.4 0.0 copy-start
  114.4 48.7 %gather_x.1 = bf16[4,8,512,128]{3,2,1,0:T(8,128)(2,1)} custom-call(bf16[8,512,128]{2,1,0:T(8,128)(2,1)} %bitcast_dynamic-update-slice_fusion.3.x_ref), custom_call_target="tpu_custom_call" | custom-call | bytes 8388608 | tf_op jit(solution)/shard_map/gather_x/pallas_call | solution.py:44
  163.2 0.0 copy-done
  163.2 1.1 bitcast_dynamic-update-slice_fusion.2
  164.2 0.0 all-to-all-done
  164.2 0.1 slice.9
  164.4 0.3 fusion.12
  164.7 0.7 fusion.7
  165.4 1.0 reshape.46.x_ref
  166.4 0.2 broadcast_in_dim_reshape.3
  166.7 54.6 %gather_z_hi.1 = bf16[2,2,128,1024]{3,2,1,0:T(8,128)(2,1)} custom-call(bf16[2,128,1024]{2,1,0:T(8,128)(2,1)} %reshape.46.x_ref), custom_call_target="tpu_custom_call" | custom-call | bytes 2097152 | tf_op jit(solution)/shard_map/gather_z_hi/pallas_call | solution.py:44
  221.3 0.8 constant_dynamic-update-slice_fusion.x_ref
  222.1 0.0 copy-start.1
  222.1 50.4 %gather_y.1 = bf16[4,2,2,128,1024]{4,3,2,1,0:T(8,128)(2,1)} custom-call(bf16[2,2,128,1024]{3,2,1,0:T(8,128)(2,1)} %constant_dynamic-update-slice_fusion.x_ref), custom_call_target="tpu_custom_call" | custom-call | bytes 8388608 | tf_op jit(solution)/shard_map/gather_y/pallas_call | solution.py:44
  272.6 0.0 copy-done.1
  272.6 1.1 bitcast_dynamic-update-slice_fusion.1.x_ref
  273.7 9.2 %gather_core.1 = bf16[2,4,2,2,128,1024]{5,4,3,2,1,0:T(8,128)(2,1)} custom-call(bf16[4,2,2,128,1024]{4,3,2,1,0:T(8,128)(2,1)} %bitcast_dynamic-update-slice_fusion.1.x_ref), custom_call_target="tpu_custom_call" | custom-call | bytes 16777216 | tf_op jit(solution)/shard_map/gather_core/pallas_call | solution.py:44
  282.9 0.0 copy-start.2
  282.9 0.0 copy-start.4
  282.9 4.9 %bitcast_dynamic-update-slice_fusion = bf16[2,4,2,2,128,1024]{5,4,3,2,1,0:T(8,128)(2,1)} fusion(bf16[2,4,2,2,128,1024]{5,4,3,2,1,0:T(8,128)(2,1)} %gather_core.1, s32[]{:T(128)S(6)} %select_n.38, bf16[4,2,2,128,1024]{4,3,2,1,0:T(8,128)(2,1)} %bitcast_dynamic-update-slice_fusion.1.x_ref), kind=kLoop, calls=%fused_computation.2 | loop fusion | bytes 8388612 | tf_op jit(solution)/shard_map/dynamic_update_slice | solution.py:57
  287.8 0.0 copy-done.2
  287.8 0.0 copy-done.4
  287.8 7.8 %bitcast_add_fusion = f32[512,1024]{1,0:T(8,128)} fusion(f32[512,1024]{1,0:T(8,128)S(1)} %copy-done.4, bf16[2,4,2,2,128,1024]{5,4,3,2,1,0:T(8,128)(2,1)} %bitcast_dynamic-update-slice_fusion, bf16[2,2,2,4,512,128]{5,4,3,2,1,0:T(8,128)(2,1)S(1)} %bitcast.37), kind=kOutput, calls=%fused_computation.4 | convolution fusion | flops 4295491584 | bytes 16777216 | tf_op jit(solution)/shard_map/ckhypj,cyhkjn->pn/dot_general | solution.py:91
  (2 shorter events, 0.0 us)
Async XLA Ops:
  1.3 112.4 %copy-start.3 = (bf16[512,128]{1,0:T(8,128)(2,1)S(1)}, bf16[512,128]{1,0:T(8,128)(2,1)}, u32[]{:S(2)}) copy-start(bf16[512,128]{1,0:T(8,128)(2,1)} %x_ref.1) | copy-start | bytes 393220
  4.9 159.4 %all-to-all-start = ((bf16[32,144,128]{2,1,0:T(8,128)(2,1)}), bf16[32,144,128]{2,1,0:T(8,128)(2,1)S(1)}, u32[]{:S(2)}, u32[]{:S(2)}) async-start(bf16[32,144,128]{2,1,0:T(8,128)(2,1)} %copy.14), calls=%async_computation | async-start | bytes 2359296 | tf_op jit(solution)/shard_map/all_to_all | solution.py:74
  114.4 48.7 %copy-start = (bf16[8,512,128]{2,1,0:T(8,128)(2,1)S(1)}, bf16[8,512,128]{2,1,0:T(8,128)(2,1)}, u32[]{:S(2)}) copy-start(bf16[8,512,128]{2,1,0:T(8,128)(2,1)} %bitcast_dynamic-update-slice_fusion.3.x_ref) | copy-start | bytes 3145732
  222.1 50.4 %copy-start.1 = (bf16[2,2,128,1024]{3,2,1,0:T(8,128)(2,1)S(1)}, bf16[2,2,128,1024]{3,2,1,0:T(8,128)(2,1)}, u32[]{:S(2)}) copy-start(bf16[2,2,128,1024]{3,2,1,0:T(8,128)(2,1)} %constant_dynamic-update-slice_fusion.x_ref) | copy-start | bytes 3145732
  282.9 4.9 %copy-start.2 = (bf16[4,8,512,128]{3,2,1,0:T(8,128)(2,1)S(1)}, bf16[4,8,512,128]{3,2,1,0:T(8,128)(2,1)}, u32[]{:S(2)}) copy-start(bf16[4,8,512,128]{3,2,1,0:T(8,128)(2,1)} %bitcast_dynamic-update-slice_fusion.2) | copy-start | bytes 12582916
  282.9 4.9 %copy-start.4 = (f32[512,1024]{1,0:T(8,128)S(1)}, f32[512,1024]{1,0:T(8,128)}, u32[]{:S(2)}) copy-start(f32[512,1024]{1,0:T(8,128)} %param.7) | copy-start | bytes 6291460

commit v4 on v1

--- a/solution.py
+++ b/solution.py
@@ -1,6 +1,10 @@
+import functools
+
 import jax
 import jax.numpy as jnp
 from jax import lax
+from jax.experimental import pallas as pl
+from jax.experimental.pallas import tpu as pltpu
 from jax.sharding import Mesh
 from jax.sharding import PartitionSpec as P
 
@@ -8,6 +12,60 @@
 COL_AXES = ("z_lo", "x")
 ROW_SPLIT = (2, 4, 2)
 COL_SPLIT = (8, 4)
+MESH = pl.DeviceIdType.MESH
+
+
+def gather_kernel(groups, *refs):
+    count = len(groups)
+    x_refs, o_refs = refs[:count], refs[count:2 * count]
+    send_sem, recv_sem = refs[2 * count:]
+    barrier = pltpu.get_barrier_semaphore()
+    for axis, n in groups:
+        me = lax.axis_index(axis)
+        for j in range(1, n):
+            peer = lax.rem(me + j, n)
+            pl.semaphore_signal(barrier, inc=1, device_id={axis: peer}, device_id_type=MESH)
+    pl.semaphore_wait(barrier, sum(n - 1 for _, n in groups))
+    copies = []
+    slot = 0
+    order = [(g, j) for j in range(1, max(n for _, n in groups)) for g in range(count) if j < groups[g][1]]
+    for g, j in order:
+        axis, n = groups[g]
+        me = lax.axis_index(axis)
+        peer = lax.rem(me + j, n)
+        copy = pltpu.make_async_remote_copy(
+            src_ref=x_refs[g],
+            dst_ref=o_refs[g].at[me],
+            send_sem=send_sem.at[slot],
+            recv_sem=recv_sem.at[slot],
+            device_id={axis: peer},
+            device_id_type=MESH,
+        )
+        copy.start()
+        copies.append(copy)
+        slot += 1
+    for copy in copies:
+        copy.wait()
+
+
+def gather(xs, groups, cid):
+    xs, groups = list(xs), list(groups)
+    slots = sum(n - 1 for _, n in groups)
+    nbytes = sum(2 * n * x.size * x.dtype.itemsize for x, (_, n) in zip(xs, groups))
+    outs = pl.pallas_call(
+        functools.partial(gather_kernel, groups),
+        out_shape=[jax.ShapeDtypeStruct((n,) + x.shape, x.dtype) for x, (_, n) in zip(xs, groups)],
+        in_specs=[pl.BlockSpec(memory_space=pl.ANY)] * len(xs),
+        out_specs=[pl.BlockSpec(memory_space=pl.ANY)] * len(xs),
+        scratch_shapes=[pltpu.SemaphoreType.DMA((slots,)), pltpu.SemaphoreType.DMA((slots,))],
+        compiler_params=pltpu.CompilerParams(collective_id=cid, has_side_effects=True),
+        cost_estimate=pl.CostEstimate(flops=0, transcendentals=0, bytes_accessed=nbytes),
+        name="gather_" + "_".join(axis for axis, _ in groups),
+    )(*xs)
+    return [
+        lax.dynamic_update_slice_in_dim(out, x[None], lax.axis_index(axis), axis=0)
+        for out, x, (axis, _) in zip(outs, xs, groups)
+    ]
 
 
 def body(amplitudes, packed_tiles, tile_ids, residual_in):
@@ -35,11 +93,10 @@
     kt = 2
     qt = per_device // kt
     block = unpacked.reshape(kt, qt, tile, tile).transpose(0, 2, 1, 3).reshape(kt, tile, qt * tile)
-    g = lax.all_gather(block, "z_hi")
-    g = lax.all_gather(g, "y")
-    g = lax.all_gather(g, "core")
-    a = lax.all_gather(amplitudes, "z_lo")
-    a = lax.all_gather(a, "x")
+    (a,) = gather([amplitudes], [("z_lo", COL_SPLIT[0])], 3)
+    (g,) = gather([block], [("z_hi", ROW_SPLIT[0])], 0)
+    a, g = gather([a, g], [("x", COL_SPLIT[1]), ("y", ROW_SPLIT[1])], 1)
+    (g,) = gather([g], [("core", ROW_SPLIT[2])], 2)
     a = a.reshape(2, 2, 2, 4, a.shape[2], a.shape[3])
     product = jnp.einsum("ckhypj,cyhkjn->pn", a, g, preferred_element_type=jnp.float32)
     return residual_in + product

time: 382 us -> 251 us (0.66)
  the two profiles are of different devices: /device:TPU:1 before, /device:TPU:97 now
where the time goes in v4:
time: 251 us; the launch traced here: 250 us
  Pallas kernels  211 us (84%)
  local copies, waits for them, and re-layouts  14.2 us (6%)
  starting transfers between devices  13.8 us (5%)
  matrix products  9.1 us (4%)
    pallas_call x4, Pallas kernels, gather(): pl.pallas_call(functools.partial(gather_kernel, groups), out_shape=[jax.S...  211 us
    all_to_all x1, starting transfers between devices, body(): lax.all_to_all(outgoing, COL_AXES, split_axis=0, concat_axis=0, tiled=True)  13.8 us
    dynamic_update_slice x5, local copies, waits for them, and re-layouts, gather(): lax.dynamic_update_slice_in_dim(out, x[None], lax.axis_index(axis), axis=0)  9.87 us
    dot_general x1, matrix products, body(): jnp.einsum('ckhypj,cyhkjn->pn', a, g, preferred_element_type=jnp.float32)  7.83 us
  transfers between devices with their start and end apart: 1, of which 0 were waited for; matrix products, arithmetic and copies ran while one was open for 0% of the time, Pallas kernels for 41%

profile of v4, /device:TPU:97, one launch (start us, length us, event | category | flops | bytes accessed | tf_op | source)
XLA Modules:
  0.0 250.3 jit_solution(11801906936457118249)
XLA Ops:
  0.0 0.7 fusion.21
  0.7 0.7 fusion.23
  1.3 0.0 copy-start.1
  1.3 1.4 copy.34
  2.8 0.1 broadcast_in_dim.11
  2.8 0.6 convolution_convert_fusion
  3.4 1.5 copy.14
  4.9 13.8 %all-to-all-start = ((bf16[32,144,128]{2,1,0:T(8,128)(2,1)}), bf16[32,144,128]{2,1,0:T(8,128)(2,1)S(1)}, u32[]{:S(2)}, u32[]{:S(2)}) async-start(bf16[32,144,128]{2,1,0:T(8,128)(2,1)} %copy.14), calls=%async_computation | async-start | bytes 2359296 | tf_op jit(solution)/shard_map/all_to_all | solution.py:85
  18.7 101.4 %gather_z_lo.1 = bf16[8,512,128]{2,1,0:T(8,128)(2,1)} custom-call(bf16[512,128]{1,0:T(8,128)(2,1)} %refs_0_.1), custom_call_target="tpu_custom_call" | custom-call | bytes 2097152 | tf_op jit(solution)/shard_map/gather_z_lo/pallas_call | solution.py:55
  120.1 0.0 copy-done.1
  120.2 0.7 bitcast_dynamic-update-slice_fusion.3.refs_0_
  120.8 0.0 all-to-all-done
  120.8 0.3 fusion.12
  121.2 0.1 slice.9
  121.3 0.7 fusion.7
  122.0 0.2 broadcast_in_dim_reshape.3
  122.2 1.0 reshape.45.refs_0_
  123.3 50.3 %gather_z_hi.1 = bf16[2,2,128,1024]{3,2,1,0:T(8,128)(2,1)} custom-call(bf16[2,128,1024]{2,1,0:T(8,128)(2,1)} %reshape.45.refs_0_), custom_call_target="tpu_custom_call" | custom-call | bytes 2097152 | tf_op jit(solution)/shard_map/gather_z_hi/pallas_call | solution.py:55
  173.6 0.8 constant_dynamic-update-slice_fusion.refs_1_
  174.4 50.2 %gather_x_y.1 = (bf16[4,8,512,128]{3,2,1,0:T(8,128)(2,1)}, bf16[4,2,2,128,1024]{4,3,2,1,0:T(8,128)(2,1)}) custom-call(bf16[8,512,128]{2,1,0:T(8,128)(2,1)} %bitcast_dynamic-update-slice_fusion.3.refs_0_, bf16[2,2,128,1024]{3,2,1,0:T(8,128)(2,1)} %constant_dynamic-update-slice_fusion.refs_1_), custom_call_target="tpu_custom_call" | custom-call | bytes 16777216 | tf_op jit(solution)/shard_map/gather_x_y/pallas_call | solution.py:55
  224.6 2.3 bitcast_dynamic-update-slice_fusion.1.refs_0_
  226.9 0.0 copy-start
  226.9 9.5 %gather_core.1 = bf16[2,4,2,2,128,1024]{5,4,3,2,1,0:T(8,128)(2,1)} custom-call(bf16[4,2,2,128,1024]{4,3,2,1,0:T(8,128)(2,1)} %bitcast_dynamic-update-slice_fusion.1.refs_0_), custom_call_target="tpu_custom_call" | custom-call | bytes 16777216 | tf_op jit(solution)/shard_map/gather_core/pallas_call | solution.py:55
  236.4 0.0 copy-done
  236.4 1.1 bitcast_dynamic-update-slice_fusion.2
  237.6 0.0 copy-start.2
  237.6 0.0 copy-start.3
  237.6 4.9 %bitcast_dynamic-update-slice_fusion = bf16[2,4,2,2,128,1024]{5,4,3,2,1,0:T(8,128)(2,1)} fusion(bf16[2,4,2,2,128,1024]{5,4,3,2,1,0:T(8,128)(2,1)} %gather_core.1, s32[]{:T(128)S(6)} %select_n.38, bf16[4,2,2,128,1024]{4,3,2,1,0:T(8,128)(2,1)} %bitcast_dynamic-update-slice_fusion.1.refs_0_), kind=kLoop, calls=%fused_computation.2 | loop fusion | bytes 8388612 | tf_op jit(solution)/shard_map/dynamic_update_slice | solution.py:66
  242.5 0.0 copy-done.2
  242.5 0.0 copy-done.3
  242.5 7.8 %bitcast_add_fusion = f32[512,1024]{1,0:T(8,128)} fusion(f32[512,1024]{1,0:T(8,128)S(1)} %copy-done.3, bf16[2,4,2,2,128,1024]{5,4,3,2,1,0:T(8,128)(2,1)} %bitcast_dynamic-update-slice_fusion, bf16[2,2,2,4,512,128]{5,4,3,2,1,0:T(8,128)(2,1)S(1)} %bitcast.38), kind=kOutput, calls=%fused_computation.4 | convolution fusion | flops 4295491584 | bytes 16777216 | tf_op jit(solution)/shard_map/ckhypj,cyhkjn->pn/dot_general | solution.py:101
  (2 shorter events, 0.0 us)
Async XLA Ops:
  1.3 118.8 %copy-start.1 = (bf16[512,128]{1,0:T(8,128)(2,1)S(1)}, bf16[512,128]{1,0:T(8,128)(2,1)}, u32[]{:S(2)}) copy-start(bf16[512,128]{1,0:T(8,128)(2,1)} %refs_0_.1) | copy-start | bytes 393220
  4.9 115.9 %all-to-all-start = ((bf16[32,144,128]{2,1,0:T(8,128)(2,1)}), bf16[32,144,128]{2,1,0:T(8,128)(2,1)S(1)}, u32[]{:S(2)}, u32[]{:S(2)}) async-start(bf16[32,144,128]{2,1,0:T(8,128)(2,1)} %copy.14), calls=%async_computation | async-start | bytes 2359296 | tf_op jit(solution)/shard_map/all_to_all | solution.py:85
  226.9 9.5 %copy-start = (bf16[8,512,128]{2,1,0:T(8,128)(2,1)S(1)}, bf16[8,512,128]{2,1,0:T(8,128)(2,1)}, u32[]{:S(2)}) copy-start(bf16[8,512,128]{2,1,0:T(8,128)(2,1)} %bitcast_dynamic-update-slice_fusion.3.refs_0_) | copy-start | bytes 3145732
  237.6 4.9 %copy-start.2 = (bf16[4,8,512,128]{3,2,1,0:T(8,128)(2,1)S(1)}, bf16[4,8,512,128]{3,2,1,0:T(8,128)(2,1)}, u32[]{:S(2)}) copy-start(bf16[4,8,512,128]{3,2,1,0:T(8,128)(2,1)} %bitcast_dynamic-update-slice_fusion.2) | copy-start | bytes 12582916
  237.6 4.9 %copy-start.3 = (f32[512,1024]{1,0:T(8,128)S(1)}, f32[512,1024]{1,0:T(8,128)}, u32[]{:S(2)}) copy-start(f32[512,1024]{1,0:T(8,128)} %param.7) | copy-start | bytes 6291460

commit v5 on v1

--- a/solution.py
+++ b/solution.py
@@ -1,6 +1,11 @@
+import functools
+import math
+
 import jax
 import jax.numpy as jnp
 from jax import lax
+from jax.experimental import pallas as pl
+from jax.experimental.pallas import tpu as pltpu
 from jax.sharding import Mesh
 from jax.sharding import PartitionSpec as P
 
@@ -8,6 +13,91 @@
 COL_AXES = ("z_lo", "x")
 ROW_SPLIT = (2, 4, 2)
 COL_SPLIT = (8, 4)
+MESH = pl.DeviceIdType.MESH
+
+
+def _index(axes, sizes):
+    index = 0
+    for axis, size in zip(axes, sizes):
+        index = index * size + lax.axis_index(axis)
+    return index
+
+
+def _device(axes, sizes, flat):
+    coords = {}
+    for axis, size in reversed(list(zip(axes, sizes))):
+        coords[axis] = lax.rem(flat, size)
+        flat = flat // size
+    return coords
+
+
+def exchange_kernel(groups, *refs):
+    count = len(groups)
+    x_refs, o_refs = refs[:count], refs[count:2 * count]
+    send_sem, recv_sem = refs[2 * count:]
+    barrier = pltpu.get_barrier_semaphore()
+    total = 0
+    for _, axes, sizes in groups:
+        n = math.prod(sizes)
+        me = _index(axes, sizes)
+        for j in range(1, n):
+            peer = _device(axes, sizes, lax.rem(me + j, n))
+            pl.semaphore_signal(barrier, inc=1, device_id=peer, device_id_type=MESH)
+        total += n - 1
+    pl.semaphore_wait(barrier, total)
+    copies = []
+    slot = 0
+    longest = max(math.prod(sizes) for _, _, sizes in groups)
+    for j in range(1, longest):
+        for g, (kind, axes, sizes) in enumerate(groups):
+            n = math.prod(sizes)
+            if j >= n:
+                continue
+            me = _index(axes, sizes)
+            flat = lax.rem(me + j, n)
+            src = x_refs[g] if kind == "gather" else x_refs[g].at[flat]
+            copy = pltpu.make_async_remote_copy(
+                src_ref=src,
+                dst_ref=o_refs[g].at[me],
+                send_sem=send_sem.at[slot],
+                recv_sem=recv_sem.at[slot],
+                device_id=_device(axes, sizes, flat),
+                device_id_type=MESH,
+            )
+            copy.start()
+            copies.append(copy)
+            slot += 1
+    for copy in copies:
+        copy.wait()
+
+
+def exchange(xs, groups, cid):
+    xs, groups = list(xs), list(groups)
+    slots = sum(math.prod(sizes) - 1 for _, _, sizes in groups)
+    shapes = []
+    for x, (kind, _, sizes) in zip(xs, groups):
+        shapes.append((math.prod(sizes),) + x.shape if kind == "gather" else x.shape)
+    nbytes = sum(2 * math.prod(shape) * x.dtype.itemsize for x, shape in zip(xs, shapes))
+    outs = pl.pallas_call(
+        functools.partial(exchange_kernel, groups),
+        out_shape=[jax.ShapeDtypeStruct(shape, x.dtype) for x, shape in zip(xs, shapes)],
+        in_specs=[pl.BlockSpec(memory_space=pl.ANY)] * len(xs),
+        out_specs=[pl.BlockSpec(memory_space=pl.ANY)] * len(xs),
+        scratch_shapes=[pltpu.SemaphoreType.DMA((slots,)), pltpu.SemaphoreType.DMA((slots,))],
+        compiler_params=pltpu.CompilerParams(collective_id=cid, has_side_effects=True),
+        cost_estimate=pl.CostEstimate(flops=0, transcendentals=0, bytes_accessed=nbytes),
+        name="exchange_" + "_".join("".join(axes) for _, axes, _ in groups),
+    )(*xs)
+    results = []
+    for out, x, (kind, axes, sizes) in zip(outs, xs, groups):
+        me = _index(axes, sizes)
+        own = x[None] if kind == "gather" else lax.dynamic_slice_in_dim(x, me, 1, axis=0)
+        results.append(lax.dynamic_update_slice_in_dim(out, own, me, axis=0))
+    return results
+
+
+def gather(xs, groups, cid):
+    return exchange(xs, [("gather", (axis,), (n,)) for axis, n in groups], cid)
 
 
 def body(amplitudes, packed_tiles, tile_ids, residual_in):
@@ -24,7 +114,11 @@
     tagged = jnp.concatenate([packed_tiles[0], tag_rows], axis=1)
     outgoing = jnp.einsum("sl,lij->sij", chooser, tagged, preferred_element_type=jnp.float32)
     outgoing = outgoing.astype(jnp.bfloat16)
-    incoming = lax.all_to_all(outgoing, COL_AXES, split_axis=0, concat_axis=0, tiled=True)
+    incoming, a = exchange(
+        [outgoing, amplitudes],
+        [("a2a", COL_AXES, COL_SPLIT), ("gather", ("z_lo",), (COL_SPLIT[0],))],
+        3,
+    )
     tags = incoming[:, tile, 0].astype(jnp.float32)
     unpack = (
         (jnp.arange(per_device, dtype=jnp.float32)[:, None] + 1.0) == tags[None, :]
@@ -35,11 +129,9 @@
     kt = 2
     qt = per_device // kt
     block = unpacked.reshape(kt, qt, tile, tile).transpose(0, 2, 1, 3).reshape(kt, tile, qt * tile)
-    g = lax.all_gather(block, "z_hi")
-    g = lax.all_gather(g, "y")
-    g = lax.all_gather(g, "core")
-    a = lax.all_gather(amplitudes, "z_lo")
-    a = lax.all_gather(a, "x")
+    (g,) = gather([block], [("z_hi", ROW_SPLIT[0])], 0)
+    a, g = gather([a, g], [("x", COL_SPLIT[1]), ("y", ROW_SPLIT[1])], 1)
+    (g,) = gather([g], [("core", ROW_SPLIT[2])], 2)
     a = a.reshape(2, 2, 2, 4, a.shape[2], a.shape[3])
     product = jnp.einsum("ckhypj,cyhkjn->pn", a, g, preferred_element_type=jnp.float32)
     return residual_in + product

time: 382 us -> 247 us (0.65)
  the two profiles are of different devices: /device:TPU:1 before, /device:TPU:225 now
where the time goes in v5:
time: 247 us; the launch traced here: 246 us
  Pallas kernels  219 us (89%)
  local copies, waits for them, and re-layouts  15.5 us (6%)
  matrix products  9.09 us (4%)
  other arithmetic  2.53 us (1%)
    pallas_call x4, Pallas kernels, exchange(): pl.pallas_call(functools.partial(exchange_kernel, groups), out_shape=[jax...  219 us
    dynamic_update_slice x6, local copies, waits for them, and re-layouts, exchange(): results.append(lax.dynamic_update_slice_in_dim(out, own, me, axis=0))  10 us
    dot_general x1, matrix products, body(): jnp.einsum('ckhypj,cyhkjn->pn', a, g, preferred_element_type=jnp.float32)  7.83 us

profile of v5, /device:TPU:225, one launch (start us, length us, event | category | flops | bytes accessed | tf_op | source)
XLA Modules:
  0.0 246.5 jit_solution(16133562964707614979)
XLA Ops:
  0.0 0.0 copy-start.2
  0.0 0.7 fusion.22
  0.7 0.7 fusion.24
  1.4 0.1 broadcast_in_dim.10
  1.5 1.4 copy.33
  2.8 0.6 fusion.9
  3.4 1.5 copy.31.refs_0_
  4.9 103.5 %exchange_z_lox_z_lo.1 = (bf16[32,144,128]{2,1,0:T(8,128)(2,1)}, bf16[8,512,128]{2,1,0:T(8,128)(2,1)}) custom-call(bf16[32,144,128]{2,1,0:T(8,128)(2,1)} %copy.31.refs_0_, bf16[512,128]{1,0:T(8,128)(2,1)} %refs_1_.1), custom_call_target="tpu_custom_call" | custom-call | bytes 4456448 | tf_op jit(solution)/shard_map/exchange_z_lox_z_lo/pallas_call | solution.py:81
  108.4 1.4 dynamic-slice_dynamic-update-slice_fusion
  109.8 0.0 copy-done.2
  109.8 0.7 bitcast_dynamic-update-slice_fusion.3.refs_0_
  110.5 1.2 fusion.13
  111.6 1.3 slice.9
  112.9 0.7 fusion.7
  113.6 0.0 copy-start.1
  113.7 0.2 broadcast_in_dim_reshape.3
  113.9 1.0 reshape.45.refs_0_
  114.9 38.4 %exchange_z_hi.1 = bf16[2,2,128,1024]{3,2,1,0:T(8,128)(2,1)} custom-call(bf16[2,128,1024]{2,1,0:T(8,128)(2,1)} %reshape.45.refs_0_), custom_call_target="tpu_custom_call" | custom-call | bytes 2097152 | tf_op jit(solution)/shard_map/exchange_z_hi/pallas_call | solution.py:81
  153.3 0.8 constant_dynamic-update-slice_fusion.refs_1_
  154.2 0.0 copy-start
  154.2 68.0 %exchange_x_y.1 = (bf16[4,8,512,128]{3,2,1,0:T(8,128)(2,1)}, bf16[4,2,2,128,1024]{4,3,2,1,0:T(8,128)(2,1)}) custom-call(bf16[8,512,128]{2,1,0:T(8,128)(2,1)} %bitcast_dynamic-update-slice_fusion.3.refs_0_, bf16[2,2,128,1024]{3,2,1,0:T(8,128)(2,1)} %constant_dynamic-update-slice_fusion.refs_1_), custom_call_target="tpu_custom_call" | custom-call | bytes 16777216 | tf_op jit(solution)/shard_map/exchange_x_y/pallas_call | solution.py:81
  222.2 0.0 copy-done.1
  222.2 1.1 bitcast_dynamic-update-slice_fusion.2
  223.3 0.0 copy-done
  223.3 1.1 bitcast_dynamic-update-slice_fusion.1.refs_0_
  224.5 9.3 %exchange_core.1 = bf16[2,4,2,2,128,1024]{5,4,3,2,1,0:T(8,128)(2,1)} custom-call(bf16[4,2,2,128,1024]{4,3,2,1,0:T(8,128)(2,1)} %bitcast_dynamic-update-slice_fusion.1.refs_0_), custom_call_target="tpu_custom_call" | custom-call | bytes 16777216 | tf_op jit(solution)/shard_map/exchange_core/pallas_call | solution.py:81
  233.7 0.0 copy-start.3
  233.7 0.0 copy-start.4
  233.7 4.9 %bitcast_dynamic-update-slice_fusion = bf16[2,4,2,2,128,1024]{5,4,3,2,1,0:T(8,128)(2,1)} fusion(bf16[2,4,2,2,128,1024]{5,4,3,2,1,0:T(8,128)(2,1)} %exchange_core.1, s32[]{:T(128)S(6)} %select_n.43, bf16[4,2,2,128,1024]{4,3,2,1,0:T(8,128)(2,1)} %bitcast_dynamic-update-slice_fusion.1.refs_0_), kind=kLoop, calls=%fused_computation.2 | loop fusion | bytes 8388612 | tf_op jit(solution)/shard_map/dynamic_update_slice | solution.py:95
  238.7 0.0 copy-done.3
  238.7 0.0 copy-done.4
  238.7 7.8 %bitcast_add_fusion = f32[512,1024]{1,0:T(8,128)} fusion(f32[512,1024]{1,0:T(8,128)S(1)} %copy-done.4, bf16[2,4,2,2,128,1024]{5,4,3,2,1,0:T(8,128)(2,1)} %bitcast_dynamic-update-slice_fusion, bf16[2,2,2,4,512,128]{5,4,3,2,1,0:T(8,128)(2,1)S(1)} %bitcast.38), kind=kOutput, calls=%fused_computation.5 | convolution fusion | flops 4295491584 | bytes 16777216 | tf_op jit(solution)/shard_map/ckhypj,cyhkjn->pn/dot_general | solution.py:136
  (2 shorter events, 0.0 us)
Async XLA Ops:
  0.0 109.8 %copy-start.2 = (bf16[512,128]{1,0:T(8,128)(2,1)S(1)}, bf16[512,128]{1,0:T(8,128)(2,1)}, u32[]{:S(2)}) copy-start(bf16[512,128]{1,0:T(8,128)(2,1)} %refs_1_.1) | copy-start | bytes 393220
  113.6 108.6 %copy-start.1 = (bf16[8,512,128]{2,1,0:T(8,128)(2,1)S(1)}, bf16[8,512,128]{2,1,0:T(8,128)(2,1)}, u32[]{:S(2)}) copy-start(bf16[8,512,128]{2,1,0:T(8,128)(2,1)} %bitcast_dynamic-update-slice_fusion.3.refs_0_) | copy-start | bytes 3145732
  154.2 69.2 %copy-start = (bf16[2,2,128,1024]{3,2,1,0:T(8,128)(2,1)S(1)}, bf16[2,2,128,1024]{3,2,1,0:T(8,128)(2,1)}, u32[]{:S(2)}) copy-start(bf16[2,2,128,1024]{3,2,1,0:T(8,128)(2,1)} %constant_dynamic-update-slice_fusion.refs_1_) | copy-start | bytes 3145732
  233.7 4.9 %copy-start.3 = (bf16[4,8,512,128]{3,2,1,0:T(8,128)(2,1)S(1)}, bf16[4,8,512,128]{3,2,1,0:T(8,128)(2,1)}, u32[]{:S(2)}) copy-start(bf16[4,8,512,128]{3,2,1,0:T(8,128)(2,1)} %bitcast_dynamic-update-slice_fusion.2) | copy-start | bytes 12582916
  233.7 4.9 %copy-start.4 = (f32[512,1024]{1,0:T(8,128)S(1)}, f32[512,1024]{1,0:T(8,128)}, u32[]{:S(2)}) copy-start(f32[512,1024]{1,0:T(8,128)} %param.7) | copy-start | bytes 6291460

commit v6 on v5

--- a/solution.py
+++ b/solution.py
@@ -34,22 +34,37 @@
 def exchange_kernel(groups, *refs):
     count = len(groups)
     x_refs, o_refs = refs[:count], refs[count:2 * count]
-    send_sem, recv_sem = refs[2 * count:]
+    send_sem, recv_sem, line_send, line_recv = refs[2 * count:]
     barrier = pltpu.get_barrier_semaphore()
     total = 0
-    for _, axes, sizes in groups:
+    for kind, axes, sizes in groups:
         n = math.prod(sizes)
+        if kind == "line":
+            axis = axes[0]
+            i = lax.axis_index(axis)
+
+            @pl.when(i > 0)
+            def _():
+                pl.semaphore_signal(barrier, inc=1, device_id={axis: i - 1}, device_id_type=MESH)
+
+            @pl.when(i < n - 1)
+            def _():
+                pl.semaphore_signal(barrier, inc=1, device_id={axis: i + 1}, device_id_type=MESH)
+
+            total = total + (i > 0).astype(jnp.int32) + (i < n - 1).astype(jnp.int32)
+            continue
         me = _index(axes, sizes)
         for j in range(1, n):
             peer = _device(axes, sizes, lax.rem(me + j, n))
             pl.semaphore_signal(barrier, inc=1, device_id=peer, device_id_type=MESH)
-        total += n - 1
+        total = total + (n - 1)
     pl.semaphore_wait(barrier, total)
     copies = []
     slot = 0
-    longest = max(math.prod(sizes) for _, _, sizes in groups)
+    direct = [(g, grp) for g, grp in enumerate(groups) if grp[0] != "line"]
+    longest = max([math.prod(sizes) for _, (_, _, sizes) in direct], default=1)
     for j in range(1, longest):
-        for g, (kind, axes, sizes) in enumerate(groups):
+        for g, (kind, axes, sizes) in direct:
             n = math.prod(sizes)
             if j >= n:
                 continue
@@ -67,23 +82,73 @@
             copy.start()
             copies.append(copy)
             slot += 1
+    for g, (kind, axes, sizes) in enumerate(groups):
+        if kind == "line":
+            _line_ring(axes[0], sizes[0], x_refs[g], o_refs[g], line_send, line_recv)
     for copy in copies:
         copy.wait()
 
 
+def _line_ring(axis, n, x_ref, o_ref, send_sem, recv_sem):
+    i = lax.axis_index(axis)
+
+    def hop(step, direction):
+        if direction == 0:
+            origin, target, alive = i - step + 1, i + 1, (i + 1 <= n - 1) & (i - step + 1 >= 0)
+        else:
+            origin, target, alive = i + step - 1, i - 1, (i >= 1) & (i + step - 1 <= n - 1)
+        origin = jnp.clip(origin, 0, n - 1)
+        src = x_ref if step == 1 else o_ref.at[origin]
+        copy = pltpu.make_async_remote_copy(
+            src_ref=src,
+            dst_ref=o_ref.at[origin],
+            send_sem=send_sem.at[direction, step - 1],
+            recv_sem=recv_sem.at[direction, step - 1],
+            device_id={axis: jnp.clip(target, 0, n - 1)},
+            device_id_type=MESH,
+        )
+        return copy, alive
+
+    def arrival(step, direction):
+        origin = i - step if direction == 0 else i + step
+        alive = (origin >= 0) & (origin <= n - 1)
+        copy = pltpu.make_async_copy(
+            x_ref, o_ref.at[jnp.clip(origin, 0, n - 1)], recv_sem.at[direction, step - 1]
+        )
+        return copy, alive
+
+    sent = []
+    for step in range(1, n):
+        for direction in (0, 1):
+            copy, alive = hop(step, direction)
+            pl.when(alive)(copy.start)
+            sent.append((copy, alive))
+        for direction in (0, 1):
+            copy, alive = arrival(step, direction)
+            pl.when(alive)(copy.wait)
+    for copy, alive in sent:
+        pl.when(alive)(copy.wait_send)
+
+
 def exchange(xs, groups, cid):
     xs, groups = list(xs), list(groups)
-    slots = sum(math.prod(sizes) - 1 for _, _, sizes in groups)
+    slots = max(1, sum(math.prod(sizes) - 1 for kind, _, sizes in groups if kind != "line"))
+    line = max([sizes[0] for kind, _, sizes in groups if kind == "line"], default=2)
     shapes = []
     for x, (kind, _, sizes) in zip(xs, groups):
-        shapes.append((math.prod(sizes),) + x.shape if kind == "gather" else x.shape)
+        shapes.append(x.shape if kind == "a2a" else (math.prod(sizes),) + x.shape)
     nbytes = sum(2 * math.prod(shape) * x.dtype.itemsize for x, shape in zip(xs, shapes))
     outs = pl.pallas_call(
         functools.partial(exchange_kernel, groups),
         out_shape=[jax.ShapeDtypeStruct(shape, x.dtype) for x, shape in zip(xs, shapes)],
         in_specs=[pl.BlockSpec(memory_space=pl.ANY)] * len(xs),
         out_specs=[pl.BlockSpec(memory_space=pl.ANY)] * len(xs),
-        scratch_shapes=[pltpu.SemaphoreType.DMA((slots,)), pltpu.SemaphoreType.DMA((slots,))],
+        scratch_shapes=[
+            pltpu.SemaphoreType.DMA((slots,)),
+            pltpu.SemaphoreType.DMA((slots,)),
+            pltpu.SemaphoreType.DMA((2, line - 1)),
+            pltpu.SemaphoreType.DMA((2, line - 1)),
+        ],
         compiler_params=pltpu.CompilerParams(collective_id=cid, has_side_effects=True),
         cost_estimate=pl.CostEstimate(flops=0, transcendentals=0, bytes_accessed=nbytes),
         name="exchange_" + "_".join("".join(axes) for _, axes, _ in groups),
@@ -91,7 +156,7 @@
     results = []
     for out, x, (kind, axes, sizes) in zip(outs, xs, groups):
         me = _index(axes, sizes)
-        own = x[None] if kind == "gather" else lax.dynamic_slice_in_dim(x, me, 1, axis=0)
+        own = lax.dynamic_slice_in_dim(x, me, 1, axis=0) if kind == "a2a" else x[None]
         results.append(lax.dynamic_update_slice_in_dim(out, own, me, axis=0))
     return results
 
@@ -116,7 +181,7 @@
     outgoing = outgoing.astype(jnp.bfloat16)
     incoming, a = exchange(
         [outgoing, amplitudes],
-        [("a2a", COL_AXES, COL_SPLIT), ("gather", ("z_lo",), (COL_SPLIT[0],))],
+        [("a2a", COL_AXES, COL_SPLIT), ("line", ("z_lo",), (COL_SPLIT[0],))],
         3,
     )
     tags = incoming[:, tile, 0].astype(jnp.float32)

time: 247 us -> 231 us (0.935)
  the two profiles are of different devices: /device:TPU:225 before, /device:TPU:65 now
where the time goes in v6:
time: 231 us
  Pallas kernels  204 us (88%)
  local copies, waits for them, and re-layouts  15.5 us (7%)
  matrix products  9.09 us (4%)
  other arithmetic  2.53 us (1%)
    pallas_call x4, Pallas kernels, exchange(): pl.pallas_call(functools.partial(exchange_kernel, groups), out_shape=[jax...  204 us
    dynamic_update_slice x6, local copies, waits for them, and re-layouts, exchange(): results.append(lax.dynamic_update_slice_in_dim(out, own, me, axis=0))  10 us
    dot_general x1, matrix products, body(): jnp.einsum('ckhypj,cyhkjn->pn', a, g, preferred_element_type=jnp.float32)  7.83 us

profile of v6, /device:TPU:65, one launch (start us, length us, event | category | flops | bytes accessed | tf_op | source)
XLA Modules:
  0.0 231.1 jit_solution(15810913353632227261)
XLA Ops:
  0.0 0.0 copy-start.2
  0.0 0.7 fusion.22
  0.7 0.7 fusion.24
  1.4 0.1 broadcast_in_dim.10
  1.5 1.4 copy.33
  2.8 0.6 fusion.9
  3.4 1.5 copy.31.refs_0_
  4.9 86.9 %exchange_z_lox_z_lo.1 = (bf16[32,144,128]{2,1,0:T(8,128)(2,1)}, bf16[8,512,128]{2,1,0:T(8,128)(2,1)}) custom-call(bf16[32,144,128]{2,1,0:T(8,128)(2,1)} %copy.31.refs_0_, bf16[512,128]{1,0:T(8,128)(2,1)} %refs_1_.1), custom_call_target="tpu_custom_call" | custom-call | bytes 4456448 | tf_op jit(solution)/shard_map/exchange_z_lox_z_lo/pallas_call | solution.py:141
  91.8 1.4 dynamic-slice_dynamic-update-slice_fusion
  93.2 0.0 copy-done.2
  93.2 0.7 bitcast_dynamic-update-slice_fusion.3.refs_0_
  93.9 1.2 fusion.13
  95.0 1.3 slice.9
  96.3 0.7 fusion.7
  97.0 0.0 copy-start.1
  97.1 0.2 broadcast_in_dim_reshape.3
  97.3 1.0 reshape.45.refs_0_
  98.3 57.1 %exchange_z_hi.1 = bf16[2,2,128,1024]{3,2,1,0:T(8,128)(2,1)} custom-call(bf16[2,128,1024]{2,1,0:T(8,128)(2,1)} %reshape.45.refs_0_), custom_call_target="tpu_custom_call" | custom-call | bytes 2097152 | tf_op jit(solution)/shard_map/exchange_z_hi/pallas_call | solution.py:141
  155.4 0.8 constant_dynamic-update-slice_fusion.refs_1_
  156.3 0.0 copy-start
  156.3 50.5 %exchange_x_y.1 = (bf16[4,8,512,128]{3,2,1,0:T(8,128)(2,1)}, bf16[4,2,2,128,1024]{4,3,2,1,0:T(8,128)(2,1)}) custom-call(bf16[8,512,128]{2,1,0:T(8,128)(2,1)} %bitcast_dynamic-update-slice_fusion.3.refs_0_, bf16[2,2,128,1024]{3,2,1,0:T(8,128)(2,1)} %constant_dynamic-update-slice_fusion.refs_1_), custom_call_target="tpu_custom_call" | custom-call | bytes 16777216 | tf_op jit(solution)/shard_map/exchange_x_y/pallas_call | solution.py:141
  206.8 0.0 copy-done.1
  206.8 1.1 bitcast_dynamic-update-slice_fusion.2
  207.9 0.0 copy-done
  207.9 1.1 bitcast_dynamic-update-slice_fusion.1.refs_0_
  209.0 9.2 %exchange_core.1 = bf16[2,4,2,2,128,1024]{5,4,3,2,1,0:T(8,128)(2,1)} custom-call(bf16[4,2,2,128,1024]{4,3,2,1,0:T(8,128)(2,1)} %bitcast_dynamic-update-slice_fusion.1.refs_0_), custom_call_target="tpu_custom_call" | custom-call | bytes 16777216 | tf_op jit(solution)/shard_map/exchange_core/pallas_call | solution.py:141
  218.3 0.0 copy-start.3
  218.3 0.0 copy-start.4
  218.3 4.9 %bitcast_dynamic-update-slice_fusion = bf16[2,4,2,2,128,1024]{5,4,3,2,1,0:T(8,128)(2,1)} fusion(bf16[2,4,2,2,128,1024]{5,4,3,2,1,0:T(8,128)(2,1)} %exchange_core.1, s32[]{:T(128)S(6)} %select_n.43, bf16[4,2,2,128,1024]{4,3,2,1,0:T(8,128)(2,1)} %bitcast_dynamic-update-slice_fusion.1.refs_0_), kind=kLoop, calls=%fused_computation.2 | loop fusion | bytes 8388612 | tf_op jit(solution)/shard_map/dynamic_update_slice | solution.py:160
  223.2 0.0 copy-done.3
  223.2 0.0 copy-done.4
  223.2 7.8 %bitcast_add_fusion = f32[512,1024]{1,0:T(8,128)} fusion(f32[512,1024]{1,0:T(8,128)S(1)} %copy-done.4, bf16[2,4,2,2,128,1024]{5,4,3,2,1,0:T(8,128)(2,1)} %bitcast_dynamic-update-slice_fusion, bf16[2,2,2,4,512,128]{5,4,3,2,1,0:T(8,128)(2,1)S(1)} %bitcast.38), kind=kOutput, calls=%fused_computation.5 | convolution fusion | flops 4295491584 | bytes 16777216 | tf_op jit(solution)/shard_map/ckhypj,cyhkjn->pn/dot_general | solution.py:201
  (2 shorter events, 0.0 us)
Async XLA Ops:
  0.0 93.2 %copy-start.2 = (bf16[512,128]{1,0:T(8,128)(2,1)S(1)}, bf16[512,128]{1,0:T(8,128)(2,1)}, u32[]{:S(2)}) copy-start(bf16[512,128]{1,0:T(8,128)(2,1)} %refs_1_.1) | copy-start | bytes 393220
  97.0 109.8 %copy-start.1 = (bf16[8,512,128]{2,1,0:T(8,128)(2,1)S(1)}, bf16[8,512,128]{2,1,0:T(8,128)(2,1)}, u32[]{:S(2)}) copy-start(bf16[8,512,128]{2,1,0:T(8,128)(2,1)} %bitcast_dynamic-update-slice_fusion.3.refs_0_) | copy-start | bytes 3145732
  156.3 51.7 %copy-start = (bf16[2,2,128,1024]{3,2,1,0:T(8,128)(2,1)S(1)}, bf16[2,2,128,1024]{3,2,1,0:T(8,128)(2,1)}, u32[]{:S(2)}) copy-start(bf16[2,2,128,1024]{3,2,1,0:T(8,128)(2,1)} %constant_dynamic-update-slice_fusion.refs_1_) | copy-start | bytes 3145732
  218.3 4.9 %copy-start.3 = (bf16[4,8,512,128]{3,2,1,0:T(8,128)(2,1)S(1)}, bf16[4,8,512,128]{3,2,1,0:T(8,128)(2,1)}, u32[]{:S(2)}) copy-start(bf16[4,8,512,128]{3,2,1,0:T(8,128)(2,1)} %bitcast_dynamic-update-slice_fusion.2) | copy-start | bytes 12582916
  218.3 4.9 %copy-start.4 = (f32[512,1024]{1,0:T(8,128)S(1)}, f32[512,1024]{1,0:T(8,128)}, u32[]{:S(2)}) copy-start(f32[512,1024]{1,0:T(8,128)} %param.7) | copy-start | bytes 6291460

commit v7 on v6

--- a/solution.py
+++ b/solution.py
@@ -165,6 +165,87 @@
     return exchange(xs, [("gather", (axis,), (n,)) for axis, n in groups], cid)
 
 
+def row_kernel(a_ref, b_ref, ao_ref, g_ref, a_send, a_recv, z_send, z_recv, y_send, y_recv, c_send, c_recv):
+    nx, ny = COL_SPLIT[1], ROW_SPLIT[1]
+    h, y, c = lax.axis_index("z_hi"), lax.axis_index("y"), lax.axis_index("core")
+    xi = lax.axis_index("x")
+    peers = [{"z_hi": 1 - h}, {"core": 1 - c}]
+    peers += [{"y": lax.rem(y + j, ny)} for j in range(1, ny)]
+    peers += [{"x": lax.rem(xi + j, nx)} for j in range(1, nx)]
+    barrier = pltpu.get_barrier_semaphore()
+    for peer in peers:
+        pl.semaphore_signal(barrier, inc=1, device_id=peer, device_id_type=MESH)
+    pl.semaphore_wait(barrier, len(peers))
+    sent = []
+
+    def send(src, dst, ssem, rsem, peer):
+        copy = pltpu.make_async_remote_copy(
+            src_ref=src, dst_ref=dst, send_sem=ssem, recv_sem=rsem, device_id=peer, device_id_type=MESH
+        )
+        copy.start()
+        sent.append(copy)
+
+    def arrive(dst, rsem, like):
+        pltpu.make_async_copy(like, dst, rsem).wait()
+
+    for j in range(1, nx):
+        send(a_ref, ao_ref.at[xi], a_send.at[j - 1], a_recv.at[j - 1], {"x": lax.rem(xi + j, nx)})
+    send(b_ref, g_ref.at[c, y, h], z_send.at[0], z_recv.at[0], {"z_hi": 1 - h})
+    for j in range(1, ny):
+        send(b_ref, g_ref.at[c, y, h], y_send.at[j - 1, 0], y_recv.at[j - 1, 0], {"y": lax.rem(y + j, ny)})
+    send(b_ref, g_ref.at[c, y, h], c_send.at[y, h], c_recv.at[y, h], {"core": 1 - c})
+    arrive(g_ref.at[c, y, 1 - h], z_recv.at[0], b_ref)
+    for j in range(1, ny):
+        src = g_ref.at[c, y, 1 - h]
+        send(src, src, y_send.at[j - 1, 1], y_recv.at[j - 1, 1], {"y": lax.rem(y + j, ny)})
+    send(g_ref.at[c, y, 1 - h], g_ref.at[c, y, 1 - h], c_send.at[y, 1 - h], c_recv.at[y, 1 - h], {"core": 1 - c})
+    for j in range(1, ny):
+        origin = lax.rem(y - j + ny, ny)
+        for k, hh in ((0, h), (1, 1 - h)):
+            block = g_ref.at[c, origin, hh]
+            arrive(block, y_recv.at[j - 1, k], b_ref)
+            send(block, block, c_send.at[origin, hh], c_recv.at[origin, hh], {"core": 1 - c})
+    for yy in range(ny):
+        for hh in range(ROW_SPLIT[0]):
+            arrive(g_ref.at[1 - c, yy, hh], c_recv.at[yy, hh], b_ref)
+    for j in range(1, nx):
+        arrive(ao_ref.at[lax.rem(xi - j + nx, nx)], a_recv.at[j - 1], a_ref)
+    for copy in sent:
+        copy.wait_send()
+
+
+def row_exchange(a, b):
+    nx = COL_SPLIT[1]
+    nh, ny, nc = ROW_SPLIT
+    a_out = (nx,) + a.shape
+    b_out = (nc, ny, nh) + b.shape
+    nbytes = 2 * (math.prod(a_out) + math.prod(b_out)) * a.dtype.itemsize
+    ao, g = pl.pallas_call(
+        row_kernel,
+        out_shape=[jax.ShapeDtypeStruct(a_out, a.dtype), jax.ShapeDtypeStruct(b_out, b.dtype)],
+        in_specs=[pl.BlockSpec(memory_space=pl.ANY)] * 2,
+        out_specs=[pl.BlockSpec(memory_space=pl.ANY)] * 2,
+        scratch_shapes=[
+            pltpu.SemaphoreType.DMA((nx - 1,)),
+            pltpu.SemaphoreType.DMA((nx - 1,)),
+            pltpu.SemaphoreType.DMA((1,)),
+            pltpu.SemaphoreType.DMA((1,)),
+            pltpu.SemaphoreType.DMA((ny - 1, 2)),
+            pltpu.SemaphoreType.DMA((ny - 1, 2)),
+            pltpu.SemaphoreType.DMA((ny, nh)),
+            pltpu.SemaphoreType.DMA((ny, nh)),
+        ],
+        compiler_params=pltpu.CompilerParams(collective_id=7, has_side_effects=True),
+        cost_estimate=pl.CostEstimate(flops=0, transcendentals=0, bytes_accessed=nbytes),
+        name="row_exchange",
+    )(a, b)
+    xi = lax.axis_index("x")
+    h, y, c = lax.axis_index("z_hi"), lax.axis_index("y"), lax.axis_index("core")
+    ao = lax.dynamic_update_slice_in_dim(ao, a[None], xi, axis=0)
+    g = lax.dynamic_update_slice(g, b[None, None, None], (c, y, h) + (0,) * b.ndim)
+    return ao, g
+
+
 def body(amplitudes, packed_tiles, tile_ids, residual_in):
     per_device = packed_tiles.shape[1]
     tile = packed_tiles.shape[2]
@@ -194,9 +275,7 @@
     kt = 2
     qt = per_device // kt
     block = unpacked.reshape(kt, qt, tile, tile).transpose(0, 2, 1, 3).reshape(kt, tile, qt * tile)
-    (g,) = gather([block], [("z_hi", ROW_SPLIT[0])], 0)
-    a, g = gather([a, g], [("x", COL_SPLIT[1]), ("y", ROW_SPLIT[1])], 1)
-    (g,) = gather([g], [("core", ROW_SPLIT[2])], 2)
+    a, g = row_exchange(a, block)
     a = a.reshape(2, 2, 2, 4, a.shape[2], a.shape[3])
     product = jnp.einsum("ckhypj,cyhkjn->pn", a, g, preferred_element_type=jnp.float32)
     return residual_in + product

time: 231 us -> 198 us (0.86)
  Pallas kernels: 204 us -> 175 us
  local copies, waits for them, and re-layouts: 15.5 us -> 9.52 us
    pallas_call x4 -> x1, Pallas kernels: 204 us -> 86.9 us  [exchange(): pl.pallas_call(functools.partial(exchange_kernel, groups), out_shape=[jax...]
    pallas_call x0 -> x1, Pallas kernels: none -> 88 us  [row_exchange(): pl.pallas_call(row_kernel, out_shape=[jax.ShapeDtypeStruct(a_out, a.dtype...]
    dynamic_update_slice x6 -> x2, local copies, waits for them, and re-layouts: 10 us -> 2.04 us  [exchange(): results.append(lax.dynamic_update_slice_in_dim(out, own, me, axis=0))]
where the time goes in v7:
time: 198 us; the launch traced here: 197 us
  Pallas kernels  175 us (88%)
  matrix products  10.4 us (5%)
  local copies, waits for them, and re-layouts  9.52 us (5%)
  other arithmetic  2.5 us (1%)
    pallas_call x1, Pallas kernels, row_exchange(): pl.pallas_call(row_kernel, out_shape=[jax.ShapeDtypeStruct(a_out, a.dtype...  88 us
    pallas_call x1, Pallas kernels, exchange(): pl.pallas_call(functools.partial(exchange_kernel, groups), out_shape=[jax...  86.9 us
    dot_general x1, matrix products, body(): jnp.einsum('ckhypj,cyhkjn->pn', a, g, preferred_element_type=jnp.float32)  9.11 us

profile of v7, /device:TPU:65, one launch (start us, length us, event | category | flops | bytes accessed | tf_op | source)
XLA Modules:
  0.0 197.4 jit_solution(15716477477541332221)
XLA Ops:
  0.0 0.7 fusion.22
  0.7 0.7 fusion.24
  1.3 0.1 broadcast_in_dim.6
  1.4 1.4 copy.33
  2.8 0.6 fusion.9
  3.4 0.0 copy-start.1
  3.4 1.5 copy.31.refs_0_
  4.9 86.9 %exchange_z_lox_z_lo.1 = (bf16[32,144,128]{2,1,0:T(8,128)(2,1)}, bf16[8,512,128]{2,1,0:T(8,128)(2,1)}) custom-call(bf16[32,144,128]{2,1,0:T(8,128)(2,1)} %copy.31.refs_0_, bf16[512,128]{1,0:T(8,128)(2,1)} %refs_1_.1), custom_call_target="tpu_custom_call" | custom-call | bytes 4456448 | tf_op jit(solution)/shard_map/exchange_z_lox_z_lo/pallas_call | solution.py:141
  91.8 1.4 dynamic-slice_dynamic-update-slice_fusion
  93.2 0.0 copy-done.1
  93.2 0.7 bitcast_dynamic-update-slice_fusion.1.a_ref
  93.9 1.2 fusion.13
  95.0 1.3 slice.9
  96.3 0.7 fusion.7
  97.0 0.0 copy-start
  97.1 0.2 broadcast_in_dim_reshape.3
  97.3 1.0 reshape.45.b_ref
  98.3 88.0 %row_exchange.1 = (bf16[4,8,512,128]{3,2,1,0:T(8,128)(2,1)}, bf16[2,4,2,2,128,1024]{5,4,3,2,1,0:T(8,128)(2,1)}) custom-call(bf16[8,512,128]{2,1,0:T(8,128)(2,1)} %bitcast_dynamic-update-slice_fusion.1.a_ref, bf16[2,128,1024]{2,1,0:T(8,128)(2,1)} %reshape.45.b_ref), custom_call_target="tpu_custom_call" | custom-call | bytes 25165824 | tf_op jit(solution)/shard_map/row_exchange/pallas_call | solution.py:223
  186.3 0.0 copy-start.2
  186.3 0.0 copy-done
  186.3 1.1 bitcast_dynamic-update-slice_fusion
  187.5 0.8 constant_dynamic-update-slice_fusion
  188.3 0.0 copy-done.2
  188.3 9.1 %bitcast_add_fusion = f32[512,1024]{1,0:T(8,128)} fusion(f32[512,1024]{1,0:T(8,128)S(1)} %copy-done.2, bf16[2,4,2,2,128,1024]{5,4,3,2,1,0:T(8,128)(2,1)} %constant_dynamic-update-slice_fusion, bf16[2,2,2,4,512,128]{5,4,3,2,1,0:T(8,128)(2,1)} %bitcast.34), kind=kOutput, calls=%fused_computation.4 | convolution fusion | flops 4295491584 | bytes 16777216 | tf_op jit(solution)/shard_map/ckhypj,cyhkjn->pn/dot_general | solution.py:280
  (2 shorter events, 0.0 us)
Async XLA Ops:
  3.4 89.8 %copy-start.1 = (bf16[512,128]{1,0:T(8,128)(2,1)S(1)}, bf16[512,128]{1,0:T(8,128)(2,1)}, u32[]{:S(2)}) copy-start(bf16[512,128]{1,0:T(8,128)(2,1)} %refs_1_.1) | copy-start | bytes 393220
  97.0 89.3 %copy-start = (bf16[8,512,128]{2,1,0:T(8,128)(2,1)S(1)}, bf16[8,512,128]{2,1,0:T(8,128)(2,1)}, u32[]{:S(2)}) copy-start(bf16[8,512,128]{2,1,0:T(8,128)(2,1)} %bitcast_dynamic-update-slice_fusion.1.a_ref) | copy-start | bytes 3145732
  186.3 2.0 %copy-start.2 = (f32[512,1024]{1,0:T(8,128)S(1)}, f32[512,1024]{1,0:T(8,128)}, u32[]{:S(2)}) copy-start(f32[512,1024]{1,0:T(8,128)} %param.7) | copy-start | bytes 6291460

commit v8 on v7

--- a/solution.py
+++ b/solution.py
@@ -165,18 +165,22 @@
     return exchange(xs, [("gather", (axis,), (n,)) for axis, n in groups], cid)
 
 
-def row_kernel(a_ref, b_ref, ao_ref, g_ref, a_send, a_recv, z_send, z_recv, y_send, y_recv, c_send, c_recv):
+def row_kernel(a_ref, b_ref, ao_ref, g_ref, *sems):
+    xd_send, xd_recv, xr_send, xr_recv, z_send, z_recv, yd_send, yd_recv, yr_send, yr_recv, c_send, c_recv = sems
     nx, ny = COL_SPLIT[1], ROW_SPLIT[1]
     h, y, c = lax.axis_index("z_hi"), lax.axis_index("y"), lax.axis_index("core")
     xi = lax.axis_index("x")
-    peers = [{"z_hi": 1 - h}, {"core": 1 - c}]
-    peers += [{"y": lax.rem(y + j, ny)} for j in range(1, ny)]
-    peers += [{"x": lax.rem(xi + j, nx)} for j in range(1, nx)]
+    up_x, dn_x, far_x = lax.rem(xi + 1, nx), lax.rem(xi + nx - 1, nx), lax.rem(xi + 2, nx)
+    up_y, dn_y, far_y = lax.rem(y + 1, ny), lax.rem(y + ny - 1, ny), lax.rem(y + 2, ny)
+    core, zpeer = {"core": 1 - c}, {"z_hi": 1 - h}
+    peers = [zpeer, core, {"y": up_y}, {"y": dn_y}, {"x": up_x}, {"x": dn_x}]
     barrier = pltpu.get_barrier_semaphore()
     for peer in peers:
         pl.semaphore_signal(barrier, inc=1, device_id=peer, device_id_type=MESH)
     pl.semaphore_wait(barrier, len(peers))
     sent = []
+    half_a = a_ref.shape[0] // 2
+    a_half = (pl.ds(0, half_a), pl.ds(half_a, half_a))
 
     def send(src, dst, ssem, rsem, peer):
         copy = pltpu.make_async_remote_copy(
@@ -188,28 +192,45 @@
     def arrive(dst, rsem, like):
         pltpu.make_async_copy(like, dst, rsem).wait()
 
-    for j in range(1, nx):
-        send(a_ref, ao_ref.at[xi], a_send.at[j - 1], a_recv.at[j - 1], {"x": lax.rem(xi + j, nx)})
-    send(b_ref, g_ref.at[c, y, h], z_send.at[0], z_recv.at[0], {"z_hi": 1 - h})
-    for j in range(1, ny):
-        send(b_ref, g_ref.at[c, y, h], y_send.at[j - 1, 0], y_recv.at[j - 1, 0], {"y": lax.rem(y + j, ny)})
-    send(b_ref, g_ref.at[c, y, h], c_send.at[y, h], c_recv.at[y, h], {"core": 1 - c})
+    def to_core(yy, hh):
+        for half in range(2):
+            block = g_ref.at[c, yy, hh, half]
+            send(block, block, c_send.at[yy, hh, half], c_recv.at[yy, hh, half], core)
+
+    send(a_ref, ao_ref.at[xi], xd_send.at[0], xd_recv.at[0], {"x": up_x})
+    send(a_ref, ao_ref.at[xi], xd_send.at[1], xd_recv.at[1], {"x": dn_x})
+    send(b_ref, g_ref.at[c, y, h], z_send.at[0], z_recv.at[0], zpeer)
+    send(b_ref, g_ref.at[c, y, h], yd_send.at[0, 0], yd_recv.at[0, 0], {"y": up_y})
+    send(b_ref, g_ref.at[c, y, h], yd_send.at[1, 0], yd_recv.at[1, 0], {"y": dn_y})
+    for half in range(2):
+        send(b_ref.at[half], g_ref.at[c, y, h, half], c_send.at[y, h, half], c_recv.at[y, h, half], core)
+    arrive(ao_ref.at[dn_x], xd_recv.at[0], a_ref)
+    src = ao_ref.at[dn_x, a_half[0]]
+    send(src, src, xr_send.at[0], xr_recv.at[0], {"x": up_x})
+    arrive(ao_ref.at[up_x], xd_recv.at[1], a_ref)
+    src = ao_ref.at[up_x, a_half[1]]
+    send(src, src, xr_send.at[1], xr_recv.at[1], {"x": dn_x})
     arrive(g_ref.at[c, y, 1 - h], z_recv.at[0], b_ref)
-    for j in range(1, ny):
-        src = g_ref.at[c, y, 1 - h]
-        send(src, src, y_send.at[j - 1, 1], y_recv.at[j - 1, 1], {"y": lax.rem(y + j, ny)})
-    send(g_ref.at[c, y, 1 - h], g_ref.at[c, y, 1 - h], c_send.at[y, 1 - h], c_recv.at[y, 1 - h], {"core": 1 - c})
-    for j in range(1, ny):
-        origin = lax.rem(y - j + ny, ny)
+    src = g_ref.at[c, y, 1 - h]
+    send(src, src, yd_send.at[0, 1], yd_recv.at[0, 1], {"y": up_y})
+    send(src, src, yd_send.at[1, 1], yd_recv.at[1, 1], {"y": dn_y})
+    to_core(y, 1 - h)
+    for direction, origin, target in ((0, dn_y, up_y), (1, up_y, dn_y)):
         for k, hh in ((0, h), (1, 1 - h)):
-            block = g_ref.at[c, origin, hh]
-            arrive(block, y_recv.at[j - 1, k], b_ref)
-            send(block, block, c_send.at[origin, hh], c_recv.at[origin, hh], {"core": 1 - c})
+            arrive(g_ref.at[c, origin, hh], yd_recv.at[direction, k], b_ref)
+            src = g_ref.at[c, origin, hh, direction]
+            send(src, src, yr_send.at[direction, k], yr_recv.at[direction, k], {"y": target})
+            to_core(origin, hh)
+    for k, hh in ((0, h), (1, 1 - h)):
+        for direction in range(2):
+            arrive(g_ref.at[c, far_y, hh, direction], yr_recv.at[direction, k], b_ref.at[0])
+        to_core(far_y, hh)
+    arrive(ao_ref.at[far_x, a_half[0]], xr_recv.at[0], a_ref.at[a_half[0]])
+    arrive(ao_ref.at[far_x, a_half[1]], xr_recv.at[1], a_ref.at[a_half[1]])
     for yy in range(ny):
         for hh in range(ROW_SPLIT[0]):
-            arrive(g_ref.at[1 - c, yy, hh], c_recv.at[yy, hh], b_ref)
-    for j in range(1, nx):
-        arrive(ao_ref.at[lax.rem(xi - j + nx, nx)], a_recv.at[j - 1], a_ref)
+            for half in range(2):
+                arrive(g_ref.at[1 - c, yy, hh, half], c_recv.at[yy, hh, half], b_ref.at[0])
     for copy in sent:
         copy.wait_send()
 
@@ -220,21 +241,13 @@
     a_out = (nx,) + a.shape
     b_out = (nc, ny, nh) + b.shape
     nbytes = 2 * (math.prod(a_out) + math.prod(b_out)) * a.dtype.itemsize
+    sem_shapes = [(2,), (2,), (1,), (2, 2), (2, 2), (ny, nh, 2)]
     ao, g = pl.pallas_call(
         row_kernel,
         out_shape=[jax.ShapeDtypeStruct(a_out, a.dtype), jax.ShapeDtypeStruct(b_out, b.dtype)],
         in_specs=[pl.BlockSpec(memory_space=pl.ANY)] * 2,
         out_specs=[pl.BlockSpec(memory_space=pl.ANY)] * 2,
-        scratch_shapes=[
-            pltpu.SemaphoreType.DMA((nx - 1,)),
-            pltpu.SemaphoreType.DMA((nx - 1,)),
-            pltpu.SemaphoreType.DMA((1,)),
-            pltpu.SemaphoreType.DMA((1,)),
-            pltpu.SemaphoreType.DMA((ny - 1, 2)),
-            pltpu.SemaphoreType.DMA((ny - 1, 2)),
-            pltpu.SemaphoreType.DMA((ny, nh)),
-            pltpu.SemaphoreType.DMA((ny, nh)),
-        ],
+        scratch_shapes=[pltpu.SemaphoreType.DMA(shape) for shape in sem_shapes for _ in range(2)],
         compiler_params=pltpu.CompilerParams(collective_id=7, has_side_effects=True),
         cost_estimate=pl.CostEstimate(flops=0, transcendentals=0, bytes_accessed=nbytes),
         name="row_exchange",

time: 198 us -> 197 us (level)
  the two profiles are of different devices: /device:TPU:65 before, /device:TPU:89 now
where the time goes in v8:
time: 197 us
  Pallas kernels  174 us (88%)
  matrix products  10.4 us (5%)
  local copies, waits for them, and re-layouts  9.52 us (5%)
  other arithmetic  2.5 us (1%)
    pallas_call x1, Pallas kernels, row_exchange(): pl.pallas_call(row_kernel, out_shape=[jax.ShapeDtypeStruct(a_out, a.dtype...  87.4 us
    pallas_call x1, Pallas kernels, exchange(): pl.pallas_call(functools.partial(exchange_kernel, groups), out_shape=[jax...  86.9 us
    dot_general x1, matrix products, body(): jnp.einsum('ckhypj,cyhkjn->pn', a, g, preferred_element_type=jnp.float32)  9.11 us

profile of v8, /device:TPU:89, one launch (start us, length us, event | category | flops | bytes accessed | tf_op | source)
XLA Modules:
  0.0 196.8 jit_solution(14438384048606964086)
XLA Ops:
  0.0 0.7 fusion.22
  0.7 0.7 fusion.24
  1.3 0.1 broadcast_in_dim.6
  1.4 1.4 copy.33
  2.8 0.6 fusion.9
  3.4 0.0 copy-start.1
  3.4 1.5 copy.31.refs_0_
  4.9 86.9 %exchange_z_lox_z_lo.1 = (bf16[32,144,128]{2,1,0:T(8,128)(2,1)}, bf16[8,512,128]{2,1,0:T(8,128)(2,1)}) custom-call(bf16[32,144,128]{2,1,0:T(8,128)(2,1)} %copy.31.refs_0_, bf16[512,128]{1,0:T(8,128)(2,1)} %refs_1_.1), custom_call_target="tpu_custom_call" | custom-call | bytes 4456448 | tf_op jit(solution)/shard_map/exchange_z_lox_z_lo/pallas_call | solution.py:141
  91.8 1.4 dynamic-slice_dynamic-update-slice_fusion
  93.2 0.0 copy-done.1
  93.2 0.7 bitcast_dynamic-update-slice_fusion.1.a_ref
  93.9 1.2 fusion.13
  95.0 1.3 slice.9
  96.3 0.7 fusion.7
  97.1 0.0 copy-start
  97.1 0.2 broadcast_in_dim_reshape.3
  97.3 1.0 reshape.45.b_ref
  98.3 87.4 %row_exchange.1 = (bf16[4,8,512,128]{3,2,1,0:T(8,128)(2,1)}, bf16[2,4,2,2,128,1024]{5,4,3,2,1,0:T(8,128)(2,1)}) custom-call(bf16[8,512,128]{2,1,0:T(8,128)(2,1)} %bitcast_dynamic-update-slice_fusion.1.a_ref, bf16[2,128,1024]{2,1,0:T(8,128)(2,1)} %reshape.45.b_ref), custom_call_target="tpu_custom_call" | custom-call | bytes 25165824 | tf_op jit(solution)/shard_map/row_exchange/pallas_call | solution.py:245
  185.7 0.0 copy-start.2
  185.7 0.0 copy-done
  185.7 1.1 bitcast_dynamic-update-slice_fusion
  186.9 0.8 constant_dynamic-update-slice_fusion
  187.7 0.0 copy-done.2
  187.7 9.1 %bitcast_add_fusion = f32[512,1024]{1,0:T(8,128)} fusion(f32[512,1024]{1,0:T(8,128)S(1)} %copy-done.2, bf16[2,4,2,2,128,1024]{5,4,3,2,1,0:T(8,128)(2,1)} %constant_dynamic-update-slice_fusion, bf16[2,2,2,4,512,128]{5,4,3,2,1,0:T(8,128)(2,1)} %bitcast.34), kind=kOutput, calls=%fused_computation.4 | convolution fusion | flops 4295491584 | bytes 16777216 | tf_op jit(solution)/shard_map/ckhypj,cyhkjn->pn/dot_general | solution.py:293
  (2 shorter events, 0.0 us)
Async XLA Ops:
  3.4 89.8 %copy-start.1 = (bf16[512,128]{1,0:T(8,128)(2,1)S(1)}, bf16[512,128]{1,0:T(8,128)(2,1)}, u32[]{:S(2)}) copy-start(bf16[512,128]{1,0:T(8,128)(2,1)} %refs_1_.1) | copy-start | bytes 393220
  97.1 88.7 %copy-start = (bf16[8,512,128]{2,1,0:T(8,128)(2,1)S(1)}, bf16[8,512,128]{2,1,0:T(8,128)(2,1)}, u32[]{:S(2)}) copy-start(bf16[8,512,128]{2,1,0:T(8,128)(2,1)} %bitcast_dynamic-update-slice_fusion.1.a_ref) | copy-start | bytes 3145732
  185.7 2.0 %copy-start.2 = (f32[512,1024]{1,0:T(8,128)S(1)}, f32[512,1024]{1,0:T(8,128)}, u32[]{:S(2)}) copy-start(f32[512,1024]{1,0:T(8,128)} %param.7) | copy-start | bytes 6291460

commit v9 on v8

--- a/solution.py
+++ b/solution.py
@@ -265,25 +265,21 @@
     col_count = COL_SPLIT[0] * COL_SPLIT[1]
     own_ids = tile_ids[0]
     target_col = own_ids // per_device
-    position = own_ids % per_device
     chooser = (jnp.arange(col_count)[:, None] == target_col[None, :]).astype(jnp.bfloat16)
-    tag_rows = jnp.broadcast_to(
-        (position + 1).astype(jnp.bfloat16)[:, None, None], (per_device, 16, tile)
-    )
-    tagged = jnp.concatenate([packed_tiles[0], tag_rows], axis=1)
-    outgoing = jnp.einsum("sl,lij->sij", chooser, tagged, preferred_element_type=jnp.float32)
+    outgoing = jnp.einsum("sl,lij->sij", chooser, packed_tiles[0], preferred_element_type=jnp.float32)
     outgoing = outgoing.astype(jnp.bfloat16)
-    incoming, a = exchange(
-        [outgoing, amplitudes],
-        [("a2a", COL_AXES, COL_SPLIT), ("line", ("z_lo",), (COL_SPLIT[0],))],
+    incoming, a, all_ids = exchange(
+        [outgoing, amplitudes, tile_ids],
+        [("a2a", COL_AXES, COL_SPLIT), ("line", ("z_lo",), (COL_SPLIT[0],)), ("gather", COL_AXES, COL_SPLIT)],
         3,
     )
-    tags = incoming[:, tile, 0].astype(jnp.float32)
-    unpack = (
-        (jnp.arange(per_device, dtype=jnp.float32)[:, None] + 1.0) == tags[None, :]
-    ).astype(jnp.bfloat16)
+    me = _index(COL_AXES, COL_SPLIT)
+    all_ids = all_ids.reshape(col_count, per_device)
+    mine = (all_ids // per_device) == me
+    tags = jnp.sum(jnp.where(mine, all_ids % per_device + 1, 0), axis=1)
+    unpack = (jnp.arange(per_device)[:, None] + 1 == tags[None, :]).astype(jnp.bfloat16)
     unpacked = jnp.einsum(
-        "ps,sij->pij", unpack, incoming[:, :tile, :], preferred_element_type=jnp.float32
+        "ps,sij->pij", unpack, incoming, preferred_element_type=jnp.float32
     ).astype(jnp.bfloat16)
     kt = 2
     qt = per_device // kt

time: 197 us -> 194 us (0.985)
  Pallas kernels: 174 us -> 171 us
    pallas_call x1, Pallas kernels: 86.9 us -> 83.3 us  [exchange(): pl.pallas_call(functools.partial(exchange_kernel, groups), out_shape=[jax...]
where the time goes in v9:
time: 194 us; the launch traced here: 193 us
  Pallas kernels  171 us (88%)
  matrix products  11.9 us (6%)
  local copies, waits for them, and re-layouts  9.09 us (5%)
    pallas_call x1, Pallas kernels, row_exchange(): pl.pallas_call(row_kernel, out_shape=[jax.ShapeDtypeStruct(a_out, a.dtype...  87.4 us
    pallas_call x1, Pallas kernels, exchange(): pl.pallas_call(functools.partial(exchange_kernel, groups), out_shape=[jax...  83.3 us
    dot_general x1, matrix products, body(): jnp.einsum('ckhypj,cyhkjn->pn', a, g, preferred_element_type=jnp.float32)  9.43 us

profile of v9, /device:TPU:89, one launch (start us, length us, event | category | flops | bytes accessed | tf_op | source)
XLA Modules:
  0.0 193.3 jit_solution(12562159206463504535)
XLA Ops:
  0.0 0.0 copy-start
  0.0 0.0 copy-start.3
  0.0 0.0 copy-start.2
  0.0 1.1 copy-done
  1.1 0.7 fusion.24
  1.8 0.6 fusion.9
  2.4 1.4 copy.26.refs_0_
  3.8 83.3 %exchange_z_lox_z_lo_z_lox.1 = (bf16[32,128,128]{2,1,0:T(8,128)(2,1)}, bf16[8,512,128]{2,1,0:T(8,128)(2,1)}, s32[32,1,16]{2,1,0:T(1,128)}) custom-call(bf16[32,128,128]{2,1,0:T(8,128)(2,1)} %copy.26.refs_0_, bf16[512,128]{1,0:T(8,128)(2,1)} %refs_1_.1, s32[1,16]{1,0:T(1,128)} %refs_2_.1), custom_call_target="tpu_custom_call" | custom-call | bytes 4198400 | tf_op jit(solution)/shard_map/exchange_z_lox_z_lo_z_lox/pallas_call | solution.py:141
  87.1 1.4 dynamic-slice_dynamic-update-slice_fusion
  88.4 0.0 copy-done.2
  88.4 0.7 bitcast_dynamic-update-slice_fusion.1.a_ref
  89.1 0.0 copy-start.1
  89.1 0.0 copy-done.3
  89.1 1.4 dynamic_update_slice.17
  90.5 0.8 fusion.14
  91.3 1.9 fusion.7
  93.3 0.2 broadcast_in_dim_reshape.3
  93.5 1.0 reshape.23.b_ref
  94.5 87.4 %row_exchange.1 = (bf16[4,8,512,128]{3,2,1,0:T(8,128)(2,1)}, bf16[2,4,2,2,128,1024]{5,4,3,2,1,0:T(8,128)(2,1)}) custom-call(bf16[8,512,128]{2,1,0:T(8,128)(2,1)} %bitcast_dynamic-update-slice_fusion.1.a_ref, bf16[2,128,1024]{2,1,0:T(8,128)(2,1)} %reshape.23.b_ref), custom_call_target="tpu_custom_call" | custom-call | bytes 25165824 | tf_op jit(solution)/shard_map/row_exchange/pallas_call | solution.py:245
  181.9 0.0 copy-done.1
  181.9 1.1 bitcast_dynamic-update-slice_fusion
  183.0 0.8 constant_dynamic-update-slice_fusion
  183.9 9.4 %bitcast_add_fusion = f32[512,1024]{1,0:T(8,128)} fusion(f32[512,1024]{1,0:T(8,128)} %param.7, bf16[2,4,2,2,128,1024]{5,4,3,2,1,0:T(8,128)(2,1)} %constant_dynamic-update-slice_fusion, bf16[2,2,2,4,512,128]{5,4,3,2,1,0:T(8,128)(2,1)} %bitcast.32), kind=kOutput, calls=%fused_computation.3 | convolution fusion | flops 4295491584 | bytes 16777216 | tf_op jit(solution)/shard_map/ckhypj,cyhkjn->pn/dot_general | solution.py:289
  (2 shorter events, 0.0 us)
Async XLA Ops:
  0.0 1.1 copy-start
  0.0 89.1 %copy-start.3 = (s32[1,16]{1,0:T(1,128)S(1)}, s32[1,16]{1,0:T(1,128)}, u32[]{:S(2)}) copy-start(s32[1,16]{1,0:T(1,128)} %refs_2_.1) | copy-start | bytes 196
  0.0 88.4 %copy-start.2 = (bf16[512,128]{1,0:T(8,128)(2,1)S(1)}, bf16[512,128]{1,0:T(8,128)(2,1)}, u32[]{:S(2)}) copy-start(bf16[512,128]{1,0:T(8,128)(2,1)} %refs_1_.1) | copy-start | bytes 393220
  89.1 92.8 %copy-start.1 = (bf16[8,512,128]{2,1,0:T(8,128)(2,1)S(1)}, bf16[8,512,128]{2,1,0:T(8,128)(2,1)}, u32[]{:S(2)}) copy-start(bf16[8,512,128]{2,1,0:T(8,128)(2,1)} %bitcast_dynamic-update-slice_fusion.1.a_ref) | copy-start | bytes 3145732

commit v10 on v9

--- a/solution.py
+++ b/solution.py
@@ -165,15 +165,22 @@
     return exchange(xs, [("gather", (axis,), (n,)) for axis, n in groups], cid)
 
 
-def row_kernel(a_ref, b_ref, ao_ref, g_ref, *sems):
+def row_kernel(a_ref, b_ref, ao_ref, g_ref, relay_ref, *sems):
     xd_send, xd_recv, xr_send, xr_recv, z_send, z_recv, yd_send, yd_recv, yr_send, yr_recv, c_send, c_recv = sems
     nx, ny = COL_SPLIT[1], ROW_SPLIT[1]
     h, y, c = lax.axis_index("z_hi"), lax.axis_index("y"), lax.axis_index("core")
     xi = lax.axis_index("x")
     up_x, dn_x, far_x = lax.rem(xi + 1, nx), lax.rem(xi + nx - 1, nx), lax.rem(xi + 2, nx)
     up_y, dn_y, far_y = lax.rem(y + 1, ny), lax.rem(y + ny - 1, ny), lax.rem(y + 2, ny)
-    core, zpeer = {"core": 1 - c}, {"z_hi": 1 - h}
-    peers = [zpeer, core, {"y": up_y}, {"y": dn_y}, {"x": up_x}, {"x": dn_x}]
+    core = {"core": 1 - c}
+    zl, nzl = lax.axis_index("z_lo"), COL_SPLIT[0]
+    quarter = nzl // 2
+    low = zl < quarter
+    up_h = jnp.where(low, h, 1 - h)
+    dn_h = jnp.where(low, 1 - h, h)
+    up_z = {"z_hi": up_h, "z_lo": jnp.where(low, zl + quarter, zl - quarter)}
+    dn_z = {"z_hi": dn_h, "z_lo": jnp.where(low, zl + quarter, zl - quarter)}
+    peers = [up_z, dn_z, core, {"y": up_y}, {"y": dn_y}, {"x": up_x}, {"x": dn_x}]
     barrier = pltpu.get_barrier_semaphore()
     for peer in peers:
         pl.semaphore_signal(barrier, inc=1, device_id=peer, device_id_type=MESH)
@@ -199,7 +206,8 @@
 
     send(a_ref, ao_ref.at[xi], xd_send.at[0], xd_recv.at[0], {"x": up_x})
     send(a_ref, ao_ref.at[xi], xd_send.at[1], xd_recv.at[1], {"x": dn_x})
-    send(b_ref, g_ref.at[c, y, h], z_send.at[0], z_recv.at[0], zpeer)
+    send(b_ref.at[0], relay_ref.at[0], z_send.at[0], z_recv.at[0], up_z)
+    send(b_ref.at[1], relay_ref.at[1], z_send.at[1], z_recv.at[1], dn_z)
     send(b_ref, g_ref.at[c, y, h], yd_send.at[0, 0], yd_recv.at[0, 0], {"y": up_y})
     send(b_ref, g_ref.at[c, y, h], yd_send.at[1, 0], yd_recv.at[1, 0], {"y": dn_y})
     for half in range(2):
@@ -210,7 +218,12 @@
     arrive(ao_ref.at[up_x], xd_recv.at[1], a_ref)
     src = ao_ref.at[up_x, a_half[1]]
     send(src, src, xr_send.at[1], xr_recv.at[1], {"x": dn_x})
-    arrive(g_ref.at[c, y, 1 - h], z_recv.at[0], b_ref)
+    arrive(relay_ref.at[0], z_recv.at[0], b_ref.at[0])
+    send(relay_ref.at[0], g_ref.at[c, y, 1 - up_h, 0], z_send.at[2], z_recv.at[2], up_z)
+    arrive(relay_ref.at[1], z_recv.at[1], b_ref.at[1])
+    send(relay_ref.at[1], g_ref.at[c, y, 1 - dn_h, 1], z_send.at[3], z_recv.at[3], dn_z)
+    arrive(g_ref.at[c, y, 1 - h, 0], z_recv.at[2], b_ref.at[0])
+    arrive(g_ref.at[c, y, 1 - h, 1], z_recv.at[3], b_ref.at[1])
     src = g_ref.at[c, y, 1 - h]
     send(src, src, yd_send.at[0, 1], yd_recv.at[0, 1], {"y": up_y})
     send(src, src, yd_send.at[1, 1], yd_recv.at[1, 1], {"y": dn_y})
@@ -241,12 +254,16 @@
     a_out = (nx,) + a.shape
     b_out = (nc, ny, nh) + b.shape
     nbytes = 2 * (math.prod(a_out) + math.prod(b_out)) * a.dtype.itemsize
-    sem_shapes = [(2,), (2,), (1,), (2, 2), (2, 2), (ny, nh, 2)]
-    ao, g = pl.pallas_call(
+    sem_shapes = [(2,), (2,), (4,), (2, 2), (2, 2), (ny, nh, 2)]
+    ao, g, _ = pl.pallas_call(
         row_kernel,
-        out_shape=[jax.ShapeDtypeStruct(a_out, a.dtype), jax.ShapeDtypeStruct(b_out, b.dtype)],
+        out_shape=[
+            jax.ShapeDtypeStruct(a_out, a.dtype),
+            jax.ShapeDtypeStruct(b_out, b.dtype),
+            jax.ShapeDtypeStruct(b.shape, b.dtype),
+        ],
         in_specs=[pl.BlockSpec(memory_space=pl.ANY)] * 2,
-        out_specs=[pl.BlockSpec(memory_space=pl.ANY)] * 2,
+        out_specs=[pl.BlockSpec(memory_space=pl.ANY)] * 3,
         scratch_shapes=[pltpu.SemaphoreType.DMA(shape) for shape in sem_shapes for _ in range(2)],
         compiler_params=pltpu.CompilerParams(collective_id=7, has_side_effects=True),
         cost_estimate=pl.CostEstimate(flops=0, transcendentals=0, bytes_accessed=nbytes),

time: 194 us -> 200 us (1.031)
  the two profiles are of different devices: /device:TPU:89 before, /device:TPU:25 now
where the time goes in v10:
time: 200 us
  Pallas kernels  177 us (88%)
  matrix products  11.9 us (6%)
  local copies, waits for them, and re-layouts  9.08 us (5%)
    pallas_call x1, Pallas kernels, exchange(): pl.pallas_call(functools.partial(exchange_kernel, groups), out_shape=[jax...  90.6 us
    pallas_call x1, Pallas kernels, row_exchange(): pl.pallas_call(row_kernel, out_shape=[jax.ShapeDtypeStruct(a_out, a.dtype...  86.9 us
    dot_general x1, matrix products, body(): jnp.einsum('ckhypj,cyhkjn->pn', a, g, preferred_element_type=jnp.float32)  9.43 us

profile of v10, /device:TPU:25, one launch (start us, length us, event | category | flops | bytes accessed | tf_op | source)
XLA Modules:
  0.0 200.1 jit_solution(17529408245206289249)
XLA Ops:
  0.0 0.0 copy-start
  0.0 0.0 copy-start.3
  0.0 0.0 copy-start.2
  0.0 1.1 copy-done
  1.1 0.7 fusion.24
  1.8 0.6 fusion.9
  2.4 1.4 copy.26.refs_0_
  3.8 90.6 %exchange_z_lox_z_lo_z_lox.1 = (bf16[32,128,128]{2,1,0:T(8,128)(2,1)}, bf16[8,512,128]{2,1,0:T(8,128)(2,1)}, s32[32,1,16]{2,1,0:T(1,128)}) custom-call(bf16[32,128,128]{2,1,0:T(8,128)(2,1)} %copy.26.refs_0_, bf16[512,128]{1,0:T(8,128)(2,1)} %refs_1_.1, s32[1,16]{1,0:T(1,128)} %refs_2_.1), custom_call_target="tpu_custom_call" | custom-call | bytes 4198400 | tf_op jit(solution)/shard_map/exchange_z_lox_z_lo_z_lox/pallas_call | solution.py:141
  94.3 1.4 dynamic-slice_dynamic-update-slice_fusion
  95.7 0.0 copy-done.2
  95.7 0.7 bitcast_dynamic-update-slice_fusion.1.a_ref
  96.4 0.0 copy-start.1
  96.4 0.0 copy-done.3
  96.4 1.4 dynamic_update_slice.17
  97.7 0.8 fusion.14
  98.6 1.9 fusion.7
  100.5 0.2 broadcast_in_dim_reshape.3
  100.8 1.0 reshape.23.b_ref
  101.8 86.9 %row_exchange.1 = (bf16[4,8,512,128]{3,2,1,0:T(8,128)(2,1)}, bf16[2,4,2,2,128,1024]{5,4,3,2,1,0:T(8,128)(2,1)}, bf16[2,128,1024]{2,1,0:T(8,128)(2,1)}) custom-call(bf16[8,512,128]{2,1,0:T(8,128)(2,1)} %bitcast_dynamic-update-slice_fusion.1.a_ref, bf16[2,128,1024]{2,1,0:T(8,128)(2,1)} %reshape.23.b_ref), custom_call_target="tpu_custom_call" | custom-call | bytes 25165824 | tf_op jit(solution)/shard_map/row_exchange/pallas_call | solution.py:258
  188.7 0.0 copy-done.1
  188.7 1.1 bitcast_dynamic-update-slice_fusion
  189.8 0.8 constant_dynamic-update-slice_fusion
  190.6 9.4 %bitcast_add_fusion = f32[512,1024]{1,0:T(8,128)} fusion(f32[512,1024]{1,0:T(8,128)} %param.7, bf16[2,4,2,2,128,1024]{5,4,3,2,1,0:T(8,128)(2,1)} %constant_dynamic-update-slice_fusion, bf16[2,2,2,4,512,128]{5,4,3,2,1,0:T(8,128)(2,1)} %bitcast.32), kind=kOutput, calls=%fused_computation.3 | convolution fusion | flops 4295491584 | bytes 16777216 | tf_op jit(solution)/shard_map/ckhypj,cyhkjn->pn/dot_general | solution.py:306
  (2 shorter events, 0.0 us)
Async XLA Ops:
  0.0 1.1 copy-start
  0.0 96.4 %copy-start.3 = (s32[1,16]{1,0:T(1,128)S(1)}, s32[1,16]{1,0:T(1,128)}, u32[]{:S(2)}) copy-start(s32[1,16]{1,0:T(1,128)} %refs_2_.1) | copy-start | bytes 196
  0.0 95.7 %copy-start.2 = (bf16[512,128]{1,0:T(8,128)(2,1)S(1)}, bf16[512,128]{1,0:T(8,128)(2,1)}, u32[]{:S(2)}) copy-start(bf16[512,128]{1,0:T(8,128)(2,1)} %refs_1_.1) | copy-start | bytes 393220
  96.4 92.3 %copy-start.1 = (bf16[8,512,128]{2,1,0:T(8,128)(2,1)S(1)}, bf16[8,512,128]{2,1,0:T(8,128)(2,1)}, u32[]{:S(2)}) copy-start(bf16[8,512,128]{2,1,0:T(8,128)(2,1)} %bitcast_dynamic-update-slice_fusion.1.a_ref) | copy-start | bytes 3145732

commit v11 on v9

--- a/solution.py
+++ b/solution.py
@@ -34,7 +34,14 @@
 def exchange_kernel(groups, *refs):
     count = len(groups)
     x_refs, o_refs = refs[:count], refs[count:2 * count]
-    send_sem, recv_sem, line_send, line_recv = refs[2 * count:]
+    send_sem, recv_sem, line_send, line_recv, local_sem = refs[2 * count:]
+    own = []
+    for g, (kind, axes, sizes) in enumerate(groups):
+        me = _index(axes, sizes)
+        src = x_refs[g].at[me] if kind == "a2a" else x_refs[g]
+        copy = pltpu.make_async_copy(src, o_refs[g].at[me], local_sem.at[g])
+        copy.start()
+        own.append(copy)
     barrier = pltpu.get_barrier_semaphore()
     total = 0
     for kind, axes, sizes in groups:
@@ -85,7 +92,7 @@
     for g, (kind, axes, sizes) in enumerate(groups):
         if kind == "line":
             _line_ring(axes[0], sizes[0], x_refs[g], o_refs[g], line_send, line_recv)
-    for copy in copies:
+    for copy in copies + own:
         copy.wait()
 
 
@@ -148,17 +155,13 @@
             pltpu.SemaphoreType.DMA((slots,)),
             pltpu.SemaphoreType.DMA((2, line - 1)),
             pltpu.SemaphoreType.DMA((2, line - 1)),
+            pltpu.SemaphoreType.DMA((len(xs),)),
         ],
         compiler_params=pltpu.CompilerParams(collective_id=cid, has_side_effects=True),
         cost_estimate=pl.CostEstimate(flops=0, transcendentals=0, bytes_accessed=nbytes),
         name="exchange_" + "_".join("".join(axes) for _, axes, _ in groups),
     )(*xs)
-    results = []
-    for out, x, (kind, axes, sizes) in zip(outs, xs, groups):
-        me = _index(axes, sizes)
-        own = lax.dynamic_slice_in_dim(x, me, 1, axis=0) if kind == "a2a" else x[None]
-        results.append(lax.dynamic_update_slice_in_dim(out, own, me, axis=0))
-    return results
+    return list(outs)
 
 
 def gather(xs, groups, cid):
@@ -166,7 +169,8 @@
 
 
 def row_kernel(a_ref, b_ref, ao_ref, g_ref, *sems):
-    xd_send, xd_recv, xr_send, xr_recv, z_send, z_recv, yd_send, yd_recv, yr_send, yr_recv, c_send, c_recv = sems
+    xd_send, xd_recv, xr_send, xr_recv, z_send, z_recv, yd_send, yd_recv, yr_send, yr_recv, c_send, c_recv = sems[:12]
+    local_sem = sems[12]
     nx, ny = COL_SPLIT[1], ROW_SPLIT[1]
     h, y, c = lax.axis_index("z_hi"), lax.axis_index("y"), lax.axis_index("core")
     xi = lax.axis_index("x")
@@ -178,6 +182,12 @@
     for peer in peers:
         pl.semaphore_signal(barrier, inc=1, device_id=peer, device_id_type=MESH)
     pl.semaphore_wait(barrier, len(peers))
+    own = [
+        pltpu.make_async_copy(a_ref, ao_ref.at[xi], local_sem.at[0]),
+        pltpu.make_async_copy(b_ref, g_ref.at[c, y, h], local_sem.at[1]),
+    ]
+    for copy in own:
+        copy.start()
     sent = []
     half_a = a_ref.shape[0] // 2
     a_half = (pl.ds(0, half_a), pl.ds(half_a, half_a))
@@ -233,6 +243,8 @@
                 arrive(g_ref.at[1 - c, yy, hh, half], c_recv.at[yy, hh, half], b_ref.at[0])
     for copy in sent:
         copy.wait_send()
+    for copy in own:
+        copy.wait()
 
 
 def row_exchange(a, b):
@@ -247,15 +259,12 @@
         out_shape=[jax.ShapeDtypeStruct(a_out, a.dtype), jax.ShapeDtypeStruct(b_out, b.dtype)],
         in_specs=[pl.BlockSpec(memory_space=pl.ANY)] * 2,
         out_specs=[pl.BlockSpec(memory_space=pl.ANY)] * 2,
-        scratch_shapes=[pltpu.SemaphoreType.DMA(shape) for shape in sem_shapes for _ in range(2)],
+        scratch_shapes=[pltpu.SemaphoreType.DMA(shape) for shape in sem_shapes for _ in range(2)]
+        + [pltpu.SemaphoreType.DMA((2,))],
         compiler_params=pltpu.CompilerParams(collective_id=7, has_side_effects=True),
         cost_estimate=pl.CostEstimate(flops=0, transcendentals=0, bytes_accessed=nbytes),
         name="row_exchange",
     )(a, b)
-    xi = lax.axis_index("x")
-    h, y, c = lax.axis_index("z_hi"), lax.axis_index("y"), lax.axis_index("core")
-    ao = lax.dynamic_update_slice_in_dim(ao, a[None], xi, axis=0)
-    g = lax.dynamic_update_slice(g, b[None, None, None], (c, y, h) + (0,) * b.ndim)
     return ao, g
 
 

time: 194 us -> 188 us (0.969)
  local copies, waits for them, and re-layouts: 9.09 us -> 3.48 us
    dynamic_update_slice x5 -> x0, local copies, waits for them, and re-layouts: 5.35 us -> none  [the longest x3 3.4 us: exchange(): results.append(lax.dynamic_update_slice_in_dim(out, own, me, axis=0))]
where the time goes in v11:
time: 188 us; the launch traced here: 187 us
  Pallas kernels  171 us (91%)
  matrix products  11.6 us (6%)
  local copies, waits for them, and re-layouts  3.48 us (2%)
    pallas_call x1, Pallas kernels, row_exchange(): pl.pallas_call(row_kernel, out_shape=[jax.ShapeDtypeStruct(a_out, a.dtype...  87.4 us
    pallas_call x1, Pallas kernels, exchange(): pl.pallas_call(functools.partial(exchange_kernel, groups), out_shape=[jax...  83.3 us
    dot_general x1, matrix products, body(): jnp.einsum('ckhypj,cyhkjn->pn', a, g, preferred_element_type=jnp.float32)  9.13 us

profile of v11, /device:TPU:89, one launch (start us, length us, event | category | flops | bytes accessed | tf_op | source)
XLA Modules:
  0.0 187.4 jit_solution(3228767525009583185)
XLA Ops:
  0.0 0.0 copy-start
  0.0 1.0 copy-done
  1.0 0.7 fusion.24
  1.7 0.6 fusion.9
  2.3 0.0 copy-start.1
  2.3 1.4 copy.26.refs_0_
  3.7 83.3 %exchange_z_lox_z_lo_z_lox.1 = (bf16[32,128,128]{2,1,0:T(8,128)(2,1)}, bf16[8,512,128]{2,1,0:T(8,128)(2,1)}, s32[32,1,16]{2,1,0:T(1,128)}) custom-call(bf16[32,128,128]{2,1,0:T(8,128)(2,1)} %copy.26.refs_0_, bf16[512,128]{1,0:T(8,128)(2,1)} %refs_1_.1, s32[1,16]{1,0:T(1,128)} %refs_2_.1), custom_call_target="tpu_custom_call" | custom-call | bytes 4198400 | tf_op jit(solution)/shard_map/exchange_z_lox_z_lo_z_lox/pallas_call | solution.py:148
  87.0 0.9 fusion.14
  87.9 1.9 %fusion.7 = bf16[2,8,128,128]{3,1,0,2:T(8,128)(2,1)S(1)} fusion(bf16[32,128,128]{2,1,0:T(8,128)(2,1)} %get-tuple-element.12, s32[32]{0:T(128)S(1)} %fusion.14, s32[16]{0:T(128)S(1)} %iota_add_fusion), kind=kOutput, calls=%fused_computation.6 | convolution fusion | flops 17039872 | bytes 1573056 | tf_op jit(solution)/shard_map/ps,sij->pij/dot_general | solution.py:290
  89.9 1.0 reshape.20.b_ref
  90.9 87.4 %row_exchange.1 = (bf16[4,8,512,128]{3,2,1,0:T(8,128)(2,1)}, bf16[2,4,2,2,128,1024]{5,4,3,2,1,0:T(8,128)(2,1)}) custom-call(bf16[8,512,128]{2,1,0:T(8,128)(2,1)} %get-tuple-element.10.a_ref, bf16[2,128,1024]{2,1,0:T(8,128)(2,1)} %reshape.20.b_ref), custom_call_target="tpu_custom_call" | custom-call | bytes 25165824 | tf_op jit(solution)/shard_map/row_exchange/pallas_call | solution.py:257
  178.3 0.0 copy-done.1
  178.3 9.1 %bitcast_add_fusion = f32[512,1024]{1,0:T(8,128)} fusion(f32[512,1024]{1,0:T(8,128)S(1)} %copy-done.1, bf16[2,4,2,2,128,1024]{5,4,3,2,1,0:T(8,128)(2,1)} %get-tuple-element.14, bf16[2,2,2,4,512,128]{5,4,3,2,1,0:T(8,128)(2,1)} %bitcast.25), kind=kOutput, calls=%fused_computation.3 | convolution fusion | flops 4295491584 | bytes 16777216 | tf_op jit(solution)/shard_map/ckhypj,cyhkjn->pn/dot_general | solution.py:298
  (2 shorter events, 0.0 us)
Async XLA Ops:
  0.0 1.0 copy-start
  2.3 175.9 %copy-start.1 = (f32[512,1024]{1,0:T(8,128)S(1)}, f32[512,1024]{1,0:T(8,128)}, u32[]{:S(2)}) copy-start(f32[512,1024]{1,0:T(8,128)} %param.7) | copy-start | bytes 6291460

commit v12 on v11

--- a/solution.py
+++ b/solution.py
@@ -70,6 +70,7 @@
     slot = 0
     direct = [(g, grp) for g, grp in enumerate(groups) if grp[0] != "line"]
     longest = max([math.prod(sizes) for _, (_, _, sizes) in direct], default=1)
+    starts = []
     for j in range(1, longest):
         for g, (kind, axes, sizes) in direct:
             n = math.prod(sizes)
@@ -86,17 +87,24 @@
                 device_id=_device(axes, sizes, flat),
                 device_id_type=MESH,
             )
-            copy.start()
+            starts.append(copy.start)
             copies.append(copy)
             slot += 1
-    for g, (kind, axes, sizes) in enumerate(groups):
-        if kind == "line":
-            _line_ring(axes[0], sizes[0], x_refs[g], o_refs[g], line_send, line_recv)
+    lines = [(g, grp) for g, grp in enumerate(groups) if grp[0] == "line"]
+    if lines:
+        g, (_, axes, sizes) = lines[0]
+        steps = sizes[0] - 1
+        per = -(-len(starts) // steps)
+        batches = [starts[k * per:(k + 1) * per] for k in range(steps)]
+        _line_ring(axes[0], sizes[0], x_refs[g], o_refs[g], line_send, line_recv, batches)
+    else:
+        for start in starts:
+            start()
     for copy in copies + own:
         copy.wait()
 
 
-def _line_ring(axis, n, x_ref, o_ref, send_sem, recv_sem):
+def _line_ring(axis, n, x_ref, o_ref, send_sem, recv_sem, batches):
     i = lax.axis_index(axis)
 
     def hop(step, direction):
@@ -130,6 +138,8 @@
             copy, alive = hop(step, direction)
             pl.when(alive)(copy.start)
             sent.append((copy, alive))
+        for start in batches[step - 1]:
+            start()
         for direction in (0, 1):
             copy, alive = arrival(step, direction)
             pl.when(alive)(copy.wait)

time: 188 us -> 188 us (level)
  the two profiles are of different devices: /device:TPU:89 before, /device:TPU:189 now
where the time goes in v12:
time: 188 us
  Pallas kernels  171 us (91%)
  matrix products  11.6 us (6%)
  local copies, waits for them, and re-layouts  3.48 us (2%)
    pallas_call x1, Pallas kernels, row_exchange(): pl.pallas_call(row_kernel, out_shape=[jax.ShapeDtypeStruct(a_out, a.dtype...  87.5 us
    pallas_call x1, Pallas kernels, exchange(): pl.pallas_call(functools.partial(exchange_kernel, groups), out_shape=[jax...  83.4 us
    dot_general x1, matrix products, body(): jnp.einsum('ckhypj,cyhkjn->pn', a, g, preferred_element_type=jnp.float32)  9.13 us

profile of v12, /device:TPU:189, one launch (start us, length us, event | category | flops | bytes accessed | tf_op | source)
XLA Modules:
  0.0 187.6 jit_solution(575562530226342767)
XLA Ops:
  0.0 0.0 copy-start
  0.0 1.0 copy-done
  1.0 0.7 fusion.24
  1.7 0.6 fusion.9
  2.3 0.0 copy-start.1
  2.3 1.4 copy.26.refs_0_
  3.7 83.4 %exchange_z_lox_z_lo_z_lox.1 = (bf16[32,128,128]{2,1,0:T(8,128)(2,1)}, bf16[8,512,128]{2,1,0:T(8,128)(2,1)}, s32[32,1,16]{2,1,0:T(1,128)}) custom-call(bf16[32,128,128]{2,1,0:T(8,128)(2,1)} %copy.26.refs_0_, bf16[512,128]{1,0:T(8,128)(2,1)} %refs_1_.1, s32[1,16]{1,0:T(1,128)} %refs_2_.1), custom_call_target="tpu_custom_call" | custom-call | bytes 4198400 | tf_op jit(solution)/shard_map/exchange_z_lox_z_lo_z_lox/pallas_call | solution.py:158
  87.1 0.9 fusion.14
  88.0 1.9 %fusion.7 = bf16[2,8,128,128]{3,1,0,2:T(8,128)(2,1)S(1)} fusion(bf16[32,128,128]{2,1,0:T(8,128)(2,1)} %get-tuple-element.12, s32[32]{0:T(128)S(1)} %fusion.14, s32[16]{0:T(128)S(1)} %iota_add_fusion), kind=kOutput, calls=%fused_computation.6 | convolution fusion | flops 17039872 | bytes 1573056 | tf_op jit(solution)/shard_map/ps,sij->pij/dot_general | solution.py:300
  89.9 1.0 reshape.20.b_ref
  90.9 87.5 %row_exchange.1 = (bf16[4,8,512,128]{3,2,1,0:T(8,128)(2,1)}, bf16[2,4,2,2,128,1024]{5,4,3,2,1,0:T(8,128)(2,1)}) custom-call(bf16[8,512,128]{2,1,0:T(8,128)(2,1)} %get-tuple-element.10.a_ref, bf16[2,128,1024]{2,1,0:T(8,128)(2,1)} %reshape.20.b_ref), custom_call_target="tpu_custom_call" | custom-call | bytes 25165824 | tf_op jit(solution)/shard_map/row_exchange/pallas_call | solution.py:267
  178.4 0.0 copy-done.1
  178.4 9.1 %bitcast_add_fusion = f32[512,1024]{1,0:T(8,128)} fusion(f32[512,1024]{1,0:T(8,128)S(1)} %copy-done.1, bf16[2,4,2,2,128,1024]{5,4,3,2,1,0:T(8,128)(2,1)} %get-tuple-element.14, bf16[2,2,2,4,512,128]{5,4,3,2,1,0:T(8,128)(2,1)} %bitcast.25), kind=kOutput, calls=%fused_computation.3 | convolution fusion | flops 4295491584 | bytes 16777216 | tf_op jit(solution)/shard_map/ckhypj,cyhkjn->pn/dot_general | solution.py:308
  (2 shorter events, 0.0 us)
Async XLA Ops:
  0.0 1.0 copy-start
  2.3 176.1 %copy-start.1 = (f32[512,1024]{1,0:T(8,128)S(1)}, f32[512,1024]{1,0:T(8,128)}, u32[]{:S(2)}) copy-start(f32[512,1024]{1,0:T(8,128)} %param.7) | copy-start | bytes 6291460

commit v13 on v11

--- a/solution.py
+++ b/solution.py
@@ -209,7 +209,8 @@
 
     send(a_ref, ao_ref.at[xi], xd_send.at[0], xd_recv.at[0], {"x": up_x})
     send(a_ref, ao_ref.at[xi], xd_send.at[1], xd_recv.at[1], {"x": dn_x})
-    send(b_ref, g_ref.at[c, y, h], z_send.at[0], z_recv.at[0], zpeer)
+    for half in range(2):
+        send(b_ref.at[half], g_ref.at[c, y, h, half], z_send.at[half], z_recv.at[half], zpeer)
     send(b_ref, g_ref.at[c, y, h], yd_send.at[0, 0], yd_recv.at[0, 0], {"y": up_y})
     send(b_ref, g_ref.at[c, y, h], yd_send.at[1, 0], yd_recv.at[1, 0], {"y": dn_y})
     for half in range(2):
@@ -220,11 +221,12 @@
     arrive(ao_ref.at[up_x], xd_recv.at[1], a_ref)
     src = ao_ref.at[up_x, a_half[1]]
     send(src, src, xr_send.at[1], xr_recv.at[1], {"x": dn_x})
-    arrive(g_ref.at[c, y, 1 - h], z_recv.at[0], b_ref)
-    src = g_ref.at[c, y, 1 - h]
-    send(src, src, yd_send.at[0, 1], yd_recv.at[0, 1], {"y": up_y})
-    send(src, src, yd_send.at[1, 1], yd_recv.at[1, 1], {"y": dn_y})
-    to_core(y, 1 - h)
+    for half in range(2):
+        src = g_ref.at[c, y, 1 - h, half]
+        arrive(src, z_recv.at[half], b_ref.at[half])
+        send(src, src, yd_send.at[0, 1 + half], yd_recv.at[0, 1], {"y": up_y})
+        send(src, src, yd_send.at[1, 1 + half], yd_recv.at[1, 1], {"y": dn_y})
+        send(src, src, c_send.at[y, 1 - h, half], c_recv.at[y, 1 - h, half], core)
     for direction, origin, target in ((0, dn_y, up_y), (1, up_y, dn_y)):
         for k, hh in ((0, h), (1, 1 - h)):
             arrive(g_ref.at[c, origin, hh], yd_recv.at[direction, k], b_ref)
@@ -253,7 +255,7 @@
     a_out = (nx,) + a.shape
     b_out = (nc, ny, nh) + b.shape
     nbytes = 2 * (math.prod(a_out) + math.prod(b_out)) * a.dtype.itemsize
-    sem_shapes = [(2,), (2,), (1,), (2, 2), (2, 2), (ny, nh, 2)]
+    sem_shapes = [(2,), (2,), (2,), (2, 3), (2, 2), (ny, nh, 2)]
     ao, g = pl.pallas_call(
         row_kernel,
         out_shape=[jax.ShapeDtypeStruct(a_out, a.dtype), jax.ShapeDtypeStruct(b_out, b.dtype)],

time: 188 us -> 182 us (0.968)
  Pallas kernels: 171 us -> 165 us
    pallas_call x1, Pallas kernels: 87.4 us -> 81.8 us  [row_exchange(): pl.pallas_call(row_kernel, out_shape=[jax.ShapeDtypeStruct(a_out, a.dtype...]
where the time goes in v13:
time: 182 us
  Pallas kernels  165 us (91%)
  matrix products  11.6 us (6%)
  local copies, waits for them, and re-layouts  3.48 us (2%)
    pallas_call x1, Pallas kernels, exchange(): pl.pallas_call(functools.partial(exchange_kernel, groups), out_shape=[jax...  83.3 us
    pallas_call x1, Pallas kernels, row_exchange(): pl.pallas_call(row_kernel, out_shape=[jax.ShapeDtypeStruct(a_out, a.dtype...  81.8 us
    dot_general x1, matrix products, body(): jnp.einsum('ckhypj,cyhkjn->pn', a, g, preferred_element_type=jnp.float32)  9.13 us

profile of v13, /device:TPU:89, one launch (start us, length us, event | category | flops | bytes accessed | tf_op | source)
XLA Modules:
  0.0 181.8 jit_solution(11967861825445956453)
XLA Ops:
  0.0 0.0 copy-start
  0.0 1.0 copy-done
  1.0 0.7 fusion.24
  1.7 0.6 fusion.9
  2.3 0.0 copy-start.1
  2.3 1.4 copy.26.refs_0_
  3.7 83.3 %exchange_z_lox_z_lo_z_lox.1 = (bf16[32,128,128]{2,1,0:T(8,128)(2,1)}, bf16[8,512,128]{2,1,0:T(8,128)(2,1)}, s32[32,1,16]{2,1,0:T(1,128)}) custom-call(bf16[32,128,128]{2,1,0:T(8,128)(2,1)} %copy.26.refs_0_, bf16[512,128]{1,0:T(8,128)(2,1)} %refs_1_.1, s32[1,16]{1,0:T(1,128)} %refs_2_.1), custom_call_target="tpu_custom_call" | custom-call | bytes 4198400 | tf_op jit(solution)/shard_map/exchange_z_lox_z_lo_z_lox/pallas_call | solution.py:148
  87.0 0.9 fusion.14
  87.9 1.9 %fusion.7 = bf16[2,8,128,128]{3,1,0,2:T(8,128)(2,1)S(1)} fusion(bf16[32,128,128]{2,1,0:T(8,128)(2,1)} %get-tuple-element.12, s32[32]{0:T(128)S(1)} %fusion.14, s32[16]{0:T(128)S(1)} %iota_add_fusion), kind=kOutput, calls=%fused_computation.6 | convolution fusion | flops 17039872 | bytes 1573056 | tf_op jit(solution)/shard_map/ps,sij->pij/dot_general | solution.py:292
  89.9 1.0 reshape.20.b_ref
  90.9 81.8 %row_exchange.1 = (bf16[4,8,512,128]{3,2,1,0:T(8,128)(2,1)}, bf16[2,4,2,2,128,1024]{5,4,3,2,1,0:T(8,128)(2,1)}) custom-call(bf16[8,512,128]{2,1,0:T(8,128)(2,1)} %get-tuple-element.10.a_ref, bf16[2,128,1024]{2,1,0:T(8,128)(2,1)} %reshape.20.b_ref), custom_call_target="tpu_custom_call" | custom-call | bytes 25165824 | tf_op jit(solution)/shard_map/row_exchange/pallas_call | solution.py:259
  172.7 0.0 copy-done.1
  172.7 9.1 %bitcast_add_fusion = f32[512,1024]{1,0:T(8,128)} fusion(f32[512,1024]{1,0:T(8,128)S(1)} %copy-done.1, bf16[2,4,2,2,128,1024]{5,4,3,2,1,0:T(8,128)(2,1)} %get-tuple-element.14, bf16[2,2,2,4,512,128]{5,4,3,2,1,0:T(8,128)(2,1)} %bitcast.25), kind=kOutput, calls=%fused_computation.3 | convolution fusion | flops 4295491584 | bytes 16777216 | tf_op jit(solution)/shard_map/ckhypj,cyhkjn->pn/dot_general | solution.py:300
  (2 shorter events, 0.0 us)
Async XLA Ops:
  0.0 1.0 copy-start
  2.3 170.4 %copy-start.1 = (f32[512,1024]{1,0:T(8,128)S(1)}, f32[512,1024]{1,0:T(8,128)}, u32[]{:S(2)}) copy-start(f32[512,1024]{1,0:T(8,128)} %param.7) | copy-start | bytes 6291460

commit v14 on v11

--- a/solution.py
+++ b/solution.py
@@ -170,7 +170,7 @@
 
 def row_kernel(a_ref, b_ref, ao_ref, g_ref, *sems):
     xd_send, xd_recv, xr_send, xr_recv, z_send, z_recv, yd_send, yd_recv, yr_send, yr_recv, c_send, c_recv = sems[:12]
-    local_sem = sems[12]
+    local_sem, piece_send = sems[12], sems[13]
     nx, ny = COL_SPLIT[1], ROW_SPLIT[1]
     h, y, c = lax.axis_index("z_hi"), lax.axis_index("y"), lax.axis_index("core")
     xi = lax.axis_index("x")
@@ -209,7 +209,10 @@
 
     send(a_ref, ao_ref.at[xi], xd_send.at[0], xd_recv.at[0], {"x": up_x})
     send(a_ref, ao_ref.at[xi], xd_send.at[1], xd_recv.at[1], {"x": dn_x})
-    send(b_ref, g_ref.at[c, y, h], z_send.at[0], z_recv.at[0], zpeer)
+    rows = b_ref.shape[1] // 2
+    pieces = [(kk, pl.ds(part * rows, rows)) for kk in range(2) for part in range(2)]
+    for p, (kk, span) in enumerate(pieces):
+        send(b_ref.at[kk, span], g_ref.at[c, y, h, kk, span], z_send.at[p], z_recv.at[p], zpeer)
     send(b_ref, g_ref.at[c, y, h], yd_send.at[0, 0], yd_recv.at[0, 0], {"y": up_y})
     send(b_ref, g_ref.at[c, y, h], yd_send.at[1, 0], yd_recv.at[1, 0], {"y": dn_y})
     for half in range(2):
@@ -220,11 +223,12 @@
     arrive(ao_ref.at[up_x], xd_recv.at[1], a_ref)
     src = ao_ref.at[up_x, a_half[1]]
     send(src, src, xr_send.at[1], xr_recv.at[1], {"x": dn_x})
-    arrive(g_ref.at[c, y, 1 - h], z_recv.at[0], b_ref)
-    src = g_ref.at[c, y, 1 - h]
-    send(src, src, yd_send.at[0, 1], yd_recv.at[0, 1], {"y": up_y})
-    send(src, src, yd_send.at[1, 1], yd_recv.at[1, 1], {"y": dn_y})
-    to_core(y, 1 - h)
+    for p, (kk, span) in enumerate(pieces):
+        src = g_ref.at[c, y, 1 - h, kk, span]
+        arrive(src, z_recv.at[p], b_ref.at[kk, span])
+        send(src, src, yd_send.at[0, 1 + p], yd_recv.at[0, 1], {"y": up_y})
+        send(src, src, yd_send.at[1, 1 + p], yd_recv.at[1, 1], {"y": dn_y})
+        send(src, src, piece_send.at[p], c_recv.at[y, 1 - h, kk], core)
     for direction, origin, target in ((0, dn_y, up_y), (1, up_y, dn_y)):
         for k, hh in ((0, h), (1, 1 - h)):
             arrive(g_ref.at[c, origin, hh], yd_recv.at[direction, k], b_ref)
@@ -253,14 +257,14 @@
     a_out = (nx,) + a.shape
     b_out = (nc, ny, nh) + b.shape
     nbytes = 2 * (math.prod(a_out) + math.prod(b_out)) * a.dtype.itemsize
-    sem_shapes = [(2,), (2,), (1,), (2, 2), (2, 2), (ny, nh, 2)]
+    sem_shapes = [(2,), (2,), (4,), (2, 5), (2, 2), (ny, nh, 2)]
     ao, g = pl.pallas_call(
         row_kernel,
         out_shape=[jax.ShapeDtypeStruct(a_out, a.dtype), jax.ShapeDtypeStruct(b_out, b.dtype)],
         in_specs=[pl.BlockSpec(memory_space=pl.ANY)] * 2,
         out_specs=[pl.BlockSpec(memory_space=pl.ANY)] * 2,
         scratch_shapes=[pltpu.SemaphoreType.DMA(shape) for shape in sem_shapes for _ in range(2)]
-        + [pltpu.SemaphoreType.DMA((2,))],
+        + [pltpu.SemaphoreType.DMA((2,)), pltpu.SemaphoreType.DMA((4,))],
         compiler_params=pltpu.CompilerParams(collective_id=7, has_side_effects=True),
         cost_estimate=pl.CostEstimate(flops=0, transcendentals=0, bytes_accessed=nbytes),
         name="row_exchange",

time: 188 us -> 179 us (0.952)
  Pallas kernels: 171 us -> 162 us
    pallas_call x1, Pallas kernels: 87.4 us -> 79.2 us  [row_exchange(): pl.pallas_call(row_kernel, out_shape=[jax.ShapeDtypeStruct(a_out, a.dtype...]
where the time goes in v14:
time: 179 us
  Pallas kernels  162 us (91%)
  matrix products  11.6 us (6%)
  local copies, waits for them, and re-layouts  3.48 us (2%)
    pallas_call x1, Pallas kernels, exchange(): pl.pallas_call(functools.partial(exchange_kernel, groups), out_shape=[jax...  83.3 us
    pallas_call x1, Pallas kernels, row_exchange(): pl.pallas_call(row_kernel, out_shape=[jax.ShapeDtypeStruct(a_out, a.dtype...  79.2 us
    dot_general x1, matrix products, body(): jnp.einsum('ckhypj,cyhkjn->pn', a, g, preferred_element_type=jnp.float32)  9.13 us

profile of v14, /device:TPU:89, one launch (start us, length us, event | category | flops | bytes accessed | tf_op | source)
XLA Modules:
  0.0 179.2 jit_solution(17366786635539944758)
XLA Ops:
  0.0 0.0 copy-start
  0.0 1.0 copy-done
  1.0 0.7 fusion.24
  1.7 0.6 fusion.9
  2.3 0.0 copy-start.1
  2.3 1.4 copy.26.refs_0_
  3.7 83.3 %exchange_z_lox_z_lo_z_lox.1 = (bf16[32,128,128]{2,1,0:T(8,128)(2,1)}, bf16[8,512,128]{2,1,0:T(8,128)(2,1)}, s32[32,1,16]{2,1,0:T(1,128)}) custom-call(bf16[32,128,128]{2,1,0:T(8,128)(2,1)} %copy.26.refs_0_, bf16[512,128]{1,0:T(8,128)(2,1)} %refs_1_.1, s32[1,16]{1,0:T(1,128)} %refs_2_.1), custom_call_target="tpu_custom_call" | custom-call | bytes 4198400 | tf_op jit(solution)/shard_map/exchange_z_lox_z_lo_z_lox/pallas_call | solution.py:148
  87.0 0.9 fusion.14
  87.9 1.9 %fusion.7 = bf16[2,8,128,128]{3,1,0,2:T(8,128)(2,1)S(1)} fusion(bf16[32,128,128]{2,1,0:T(8,128)(2,1)} %get-tuple-element.12, s32[32]{0:T(128)S(1)} %fusion.14, s32[16]{0:T(128)S(1)} %iota_add_fusion), kind=kOutput, calls=%fused_computation.6 | convolution fusion | flops 17039872 | bytes 1573056 | tf_op jit(solution)/shard_map/ps,sij->pij/dot_general | solution.py:294
  89.9 1.0 reshape.20.b_ref
  90.9 79.2 %row_exchange.1 = (bf16[4,8,512,128]{3,2,1,0:T(8,128)(2,1)}, bf16[2,4,2,2,128,1024]{5,4,3,2,1,0:T(8,128)(2,1)}) custom-call(bf16[8,512,128]{2,1,0:T(8,128)(2,1)} %get-tuple-element.10.a_ref, bf16[2,128,1024]{2,1,0:T(8,128)(2,1)} %reshape.20.b_ref), custom_call_target="tpu_custom_call" | custom-call | bytes 25165824 | tf_op jit(solution)/shard_map/row_exchange/pallas_call | solution.py:261
  170.1 0.0 copy-done.1
  170.1 9.1 %bitcast_add_fusion = f32[512,1024]{1,0:T(8,128)} fusion(f32[512,1024]{1,0:T(8,128)S(1)} %copy-done.1, bf16[2,4,2,2,128,1024]{5,4,3,2,1,0:T(8,128)(2,1)} %get-tuple-element.14, bf16[2,2,2,4,512,128]{5,4,3,2,1,0:T(8,128)(2,1)} %bitcast.25), kind=kOutput, calls=%fused_computation.3 | convolution fusion | flops 4295491584 | bytes 16777216 | tf_op jit(solution)/shard_map/ckhypj,cyhkjn->pn/dot_general | solution.py:302
  (2 shorter events, 0.0 us)
Async XLA Ops:
  0.0 1.0 copy-start
  2.3 167.7 %copy-start.1 = (f32[512,1024]{1,0:T(8,128)S(1)}, f32[512,1024]{1,0:T(8,128)}, u32[]{:S(2)}) copy-start(f32[512,1024]{1,0:T(8,128)} %param.7) | copy-start | bytes 6291460

commit v15 on v14

--- a/solution.py
+++ b/solution.py
@@ -170,7 +170,7 @@
 
 def row_kernel(a_ref, b_ref, ao_ref, g_ref, *sems):
     xd_send, xd_recv, xr_send, xr_recv, z_send, z_recv, yd_send, yd_recv, yr_send, yr_recv, c_send, c_recv = sems[:12]
-    local_sem, piece_send = sems[12], sems[13]
+    local_sem, piece_send, relay_send, forward_send = sems[12:16]
     nx, ny = COL_SPLIT[1], ROW_SPLIT[1]
     h, y, c = lax.axis_index("z_hi"), lax.axis_index("y"), lax.axis_index("core")
     xi = lax.axis_index("x")
@@ -226,15 +226,20 @@
     for p, (kk, span) in enumerate(pieces):
         src = g_ref.at[c, y, 1 - h, kk, span]
         arrive(src, z_recv.at[p], b_ref.at[kk, span])
-        send(src, src, yd_send.at[0, 1 + p], yd_recv.at[0, 1], {"y": up_y})
-        send(src, src, yd_send.at[1, 1 + p], yd_recv.at[1, 1], {"y": dn_y})
+        send(src, src, yd_send.at[0, 1 + p], yd_recv.at[0, 1 + p], {"y": up_y})
+        send(src, src, yd_send.at[1, 1 + p], yd_recv.at[1, 1 + p], {"y": dn_y})
         send(src, src, piece_send.at[p], c_recv.at[y, 1 - h, kk], core)
     for direction, origin, target in ((0, dn_y, up_y), (1, up_y, dn_y)):
-        for k, hh in ((0, h), (1, 1 - h)):
-            arrive(g_ref.at[c, origin, hh], yd_recv.at[direction, k], b_ref)
-            src = g_ref.at[c, origin, hh, direction]
-            send(src, src, yr_send.at[direction, k], yr_recv.at[direction, k], {"y": target})
-            to_core(origin, hh)
+        arrive(g_ref.at[c, origin, h], yd_recv.at[direction, 0], b_ref)
+        src = g_ref.at[c, origin, h, direction]
+        send(src, src, yr_send.at[direction, 0], yr_recv.at[direction, 0], {"y": target})
+        to_core(origin, h)
+        for p, (kk, span) in enumerate(pieces):
+            blk = g_ref.at[c, origin, 1 - h, kk, span]
+            arrive(blk, yd_recv.at[direction, 1 + p], b_ref.at[kk, span])
+            if kk == direction:
+                send(blk, blk, relay_send.at[direction, p % 2], yr_recv.at[direction, 1], {"y": target})
+            send(blk, blk, forward_send.at[direction, p], c_recv.at[origin, 1 - h, kk], core)
     for k, hh in ((0, h), (1, 1 - h)):
         for direction in range(2):
             arrive(g_ref.at[c, far_y, hh, direction], yr_recv.at[direction, k], b_ref.at[0])
@@ -264,7 +269,7 @@
         in_specs=[pl.BlockSpec(memory_space=pl.ANY)] * 2,
         out_specs=[pl.BlockSpec(memory_space=pl.ANY)] * 2,
         scratch_shapes=[pltpu.SemaphoreType.DMA(shape) for shape in sem_shapes for _ in range(2)]
-        + [pltpu.SemaphoreType.DMA((2,)), pltpu.SemaphoreType.DMA((4,))],
+        + [pltpu.SemaphoreType.DMA(shape) for shape in ((2,), (4,), (2, 2), (2, 4))],
         compiler_params=pltpu.CompilerParams(collective_id=7, has_side_effects=True),
         cost_estimate=pl.CostEstimate(flops=0, transcendentals=0, bytes_accessed=nbytes),
         name="row_exchange",

time: 179 us -> 180 us (level)
  no operation moved by 1% of the time
where the time goes in v15:
time: 180 us; the launch traced here: 179 us
  Pallas kernels  163 us (91%)
  matrix products  11.6 us (6%)
  local copies, waits for them, and re-layouts  3.48 us (2%)
    pallas_call x1, Pallas kernels, exchange(): pl.pallas_call(functools.partial(exchange_kernel, groups), out_shape=[jax...  83.3 us
    pallas_call x1, Pallas kernels, row_exchange(): pl.pallas_call(row_kernel, out_shape=[jax.ShapeDtypeStruct(a_out, a.dtype...  79.3 us
    dot_general x1, matrix products, body(): jnp.einsum('ckhypj,cyhkjn->pn', a, g, preferred_element_type=jnp.float32)  9.13 us

profile of v15, /device:TPU:89, one launch (start us, length us, event | category | flops | bytes accessed | tf_op | source)
XLA Modules:
  0.0 179.3 jit_solution(10614783886554992055)
XLA Ops:
  0.0 0.0 copy-start
  0.0 1.0 copy-done
  1.0 0.7 fusion.24
  1.7 0.6 fusion.9
  2.3 0.0 copy-start.1
  2.3 1.4 copy.26.refs_0_
  3.7 83.3 %exchange_z_lox_z_lo_z_lox.1 = (bf16[32,128,128]{2,1,0:T(8,128)(2,1)}, bf16[8,512,128]{2,1,0:T(8,128)(2,1)}, s32[32,1,16]{2,1,0:T(1,128)}) custom-call(bf16[32,128,128]{2,1,0:T(8,128)(2,1)} %copy.26.refs_0_, bf16[512,128]{1,0:T(8,128)(2,1)} %refs_1_.1, s32[1,16]{1,0:T(1,128)} %refs_2_.1), custom_call_target="tpu_custom_call" | custom-call | bytes 4198400 | tf_op jit(solution)/shard_map/exchange_z_lox_z_lo_z_lox/pallas_call | solution.py:148
  87.0 0.9 fusion.14
  87.9 1.9 %fusion.7 = bf16[2,8,128,128]{3,1,0,2:T(8,128)(2,1)S(1)} fusion(bf16[32,128,128]{2,1,0:T(8,128)(2,1)} %get-tuple-element.12, s32[32]{0:T(128)S(1)} %fusion.14, s32[16]{0:T(128)S(1)} %iota_add_fusion), kind=kOutput, calls=%fused_computation.6 | convolution fusion | flops 17039872 | bytes 1573056 | tf_op jit(solution)/shard_map/ps,sij->pij/dot_general | solution.py:299
  89.9 1.0 reshape.20.b_ref
  90.9 79.3 %row_exchange.1 = (bf16[4,8,512,128]{3,2,1,0:T(8,128)(2,1)}, bf16[2,4,2,2,128,1024]{5,4,3,2,1,0:T(8,128)(2,1)}) custom-call(bf16[8,512,128]{2,1,0:T(8,128)(2,1)} %get-tuple-element.10.a_ref, bf16[2,128,1024]{2,1,0:T(8,128)(2,1)} %reshape.20.b_ref), custom_call_target="tpu_custom_call" | custom-call | bytes 25165824 | tf_op jit(solution)/shard_map/row_exchange/pallas_call | solution.py:266
  170.2 0.0 copy-done.1
  170.2 9.1 %bitcast_add_fusion = f32[512,1024]{1,0:T(8,128)} fusion(f32[512,1024]{1,0:T(8,128)S(1)} %copy-done.1, bf16[2,4,2,2,128,1024]{5,4,3,2,1,0:T(8,128)(2,1)} %get-tuple-element.14, bf16[2,2,2,4,512,128]{5,4,3,2,1,0:T(8,128)(2,1)} %bitcast.25), kind=kOutput, calls=%fused_computation.3 | convolution fusion | flops 4295491584 | bytes 16777216 | tf_op jit(solution)/shard_map/ckhypj,cyhkjn->pn/dot_general | solution.py:307
  (2 shorter events, 0.0 us)
Async XLA Ops:
  0.0 1.0 copy-start
  2.3 167.9 %copy-start.1 = (f32[512,1024]{1,0:T(8,128)S(1)}, f32[512,1024]{1,0:T(8,128)}, u32[]{:S(2)}) copy-start(f32[512,1024]{1,0:T(8,128)} %param.7) | copy-start | bytes 6291460

commit v16 on v14

--- a/solution.py
+++ b/solution.py
@@ -209,8 +209,8 @@
 
     send(a_ref, ao_ref.at[xi], xd_send.at[0], xd_recv.at[0], {"x": up_x})
     send(a_ref, ao_ref.at[xi], xd_send.at[1], xd_recv.at[1], {"x": dn_x})
-    rows = b_ref.shape[1] // 2
-    pieces = [(kk, pl.ds(part * rows, rows)) for kk in range(2) for part in range(2)]
+    rows = b_ref.shape[1] // 4
+    pieces = [(kk, pl.ds(part * rows, rows)) for kk in range(2) for part in range(4)]
     for p, (kk, span) in enumerate(pieces):
         send(b_ref.at[kk, span], g_ref.at[c, y, h, kk, span], z_send.at[p], z_recv.at[p], zpeer)
     send(b_ref, g_ref.at[c, y, h], yd_send.at[0, 0], yd_recv.at[0, 0], {"y": up_y})
@@ -257,14 +257,14 @@
     a_out = (nx,) + a.shape
     b_out = (nc, ny, nh) + b.shape
     nbytes = 2 * (math.prod(a_out) + math.prod(b_out)) * a.dtype.itemsize
-    sem_shapes = [(2,), (2,), (4,), (2, 5), (2, 2), (ny, nh, 2)]
+    sem_shapes = [(2,), (2,), (8,), (2, 9), (2, 2), (ny, nh, 2)]
     ao, g = pl.pallas_call(
         row_kernel,
         out_shape=[jax.ShapeDtypeStruct(a_out, a.dtype), jax.ShapeDtypeStruct(b_out, b.dtype)],
         in_specs=[pl.BlockSpec(memory_space=pl.ANY)] * 2,
         out_specs=[pl.BlockSpec(memory_space=pl.ANY)] * 2,
         scratch_shapes=[pltpu.SemaphoreType.DMA(shape) for shape in sem_shapes for _ in range(2)]
-        + [pltpu.SemaphoreType.DMA((2,)), pltpu.SemaphoreType.DMA((4,))],
+        + [pltpu.SemaphoreType.DMA((2,)), pltpu.SemaphoreType.DMA((8,))],
         compiler_params=pltpu.CompilerParams(collective_id=7, has_side_effects=True),
         cost_estimate=pl.CostEstimate(flops=0, transcendentals=0, bytes_accessed=nbytes),
         name="row_exchange",

time: 179 us -> 178 us (level)
  no operation moved by 1% of the time
where the time goes in v16:
time: 178 us
  Pallas kernels  162 us (91%)
  matrix products  11.6 us (7%)
  local copies, waits for them, and re-layouts  3.48 us (2%)
    pallas_call x1, Pallas kernels, exchange(): pl.pallas_call(functools.partial(exchange_kernel, groups), out_shape=[jax...  83.3 us
    pallas_call x1, Pallas kernels, row_exchange(): pl.pallas_call(row_kernel, out_shape=[jax.ShapeDtypeStruct(a_out, a.dtype...  78.2 us
    dot_general x1, matrix products, body(): jnp.einsum('ckhypj,cyhkjn->pn', a, g, preferred_element_type=jnp.float32)  9.13 us

profile of v16, /device:TPU:89, one launch (start us, length us, event | category | flops | bytes accessed | tf_op | source)
XLA Modules:
  0.0 178.2 jit_solution(8847712128860287107)
XLA Ops:
  0.0 0.0 copy-start
  0.0 1.0 copy-done
  1.0 0.7 fusion.24
  1.7 0.6 fusion.9
  2.3 0.0 copy-start.1
  2.3 1.4 copy.26.refs_0_
  3.7 83.3 %exchange_z_lox_z_lo_z_lox.1 = (bf16[32,128,128]{2,1,0:T(8,128)(2,1)}, bf16[8,512,128]{2,1,0:T(8,128)(2,1)}, s32[32,1,16]{2,1,0:T(1,128)}) custom-call(bf16[32,128,128]{2,1,0:T(8,128)(2,1)} %copy.26.refs_0_, bf16[512,128]{1,0:T(8,128)(2,1)} %refs_1_.1, s32[1,16]{1,0:T(1,128)} %refs_2_.1), custom_call_target="tpu_custom_call" | custom-call | bytes 4198400 | tf_op jit(solution)/shard_map/exchange_z_lox_z_lo_z_lox/pallas_call | solution.py:148
  87.0 0.9 fusion.14
  87.9 1.9 %fusion.7 = bf16[2,8,128,128]{3,1,0,2:T(8,128)(2,1)S(1)} fusion(bf16[32,128,128]{2,1,0:T(8,128)(2,1)} %get-tuple-element.12, s32[32]{0:T(128)S(1)} %fusion.14, s32[16]{0:T(128)S(1)} %iota_add_fusion), kind=kOutput, calls=%fused_computation.6 | convolution fusion | flops 17039872 | bytes 1573056 | tf_op jit(solution)/shard_map/ps,sij->pij/dot_general | solution.py:294
  89.9 1.0 reshape.20.b_ref
  90.9 78.2 %row_exchange.1 = (bf16[4,8,512,128]{3,2,1,0:T(8,128)(2,1)}, bf16[2,4,2,2,128,1024]{5,4,3,2,1,0:T(8,128)(2,1)}) custom-call(bf16[8,512,128]{2,1,0:T(8,128)(2,1)} %get-tuple-element.10.a_ref, bf16[2,128,1024]{2,1,0:T(8,128)(2,1)} %reshape.20.b_ref), custom_call_target="tpu_custom_call" | custom-call | bytes 25165824 | tf_op jit(solution)/shard_map/row_exchange/pallas_call | solution.py:261
  169.1 0.0 copy-done.1
  169.1 9.1 %bitcast_add_fusion = f32[512,1024]{1,0:T(8,128)} fusion(f32[512,1024]{1,0:T(8,128)S(1)} %copy-done.1, bf16[2,4,2,2,128,1024]{5,4,3,2,1,0:T(8,128)(2,1)} %get-tuple-element.14, bf16[2,2,2,4,512,128]{5,4,3,2,1,0:T(8,128)(2,1)} %bitcast.25), kind=kOutput, calls=%fused_computation.3 | convolution fusion | flops 4295491584 | bytes 16777216 | tf_op jit(solution)/shard_map/ckhypj,cyhkjn->pn/dot_general | solution.py:302
  (2 shorter events, 0.0 us)
Async XLA Ops:
  0.0 1.0 copy-start
  2.3 166.7 %copy-start.1 = (f32[512,1024]{1,0:T(8,128)S(1)}, f32[512,1024]{1,0:T(8,128)}, u32[]{:S(2)}) copy-start(f32[512,1024]{1,0:T(8,128)} %param.7) | copy-start | bytes 6291460

commit v17 on v16

--- a/solution.py
+++ b/solution.py
@@ -278,9 +278,9 @@
     col_count = COL_SPLIT[0] * COL_SPLIT[1]
     own_ids = tile_ids[0]
     target_col = own_ids // per_device
-    chooser = (jnp.arange(col_count)[:, None] == target_col[None, :]).astype(jnp.bfloat16)
-    outgoing = jnp.einsum("sl,lij->sij", chooser, packed_tiles[0], preferred_element_type=jnp.float32)
-    outgoing = outgoing.astype(jnp.bfloat16)
+    chooser = jnp.arange(col_count)[:, None] == target_col[None, :]
+    source = jnp.sum(jnp.where(chooser, jnp.arange(per_device)[None, :], 0), axis=1)
+    outgoing = jnp.take(packed_tiles[0], source, axis=0)
     incoming, a, all_ids = exchange(
         [outgoing, amplitudes, tile_ids],
         [("a2a", COL_AXES, COL_SPLIT), ("line", ("z_lo",), (COL_SPLIT[0],)), ("gather", COL_AXES, COL_SPLIT)],
@@ -290,10 +290,9 @@
     all_ids = all_ids.reshape(col_count, per_device)
     mine = (all_ids // per_device) == me
     tags = jnp.sum(jnp.where(mine, all_ids % per_device + 1, 0), axis=1)
-    unpack = (jnp.arange(per_device)[:, None] + 1 == tags[None, :]).astype(jnp.bfloat16)
-    unpacked = jnp.einsum(
-        "ps,sij->pij", unpack, incoming, preferred_element_type=jnp.float32
-    ).astype(jnp.bfloat16)
+    holds = jnp.arange(per_device)[:, None] + 1 == tags[None, :]
+    slot_of = jnp.sum(jnp.where(holds, jnp.arange(col_count)[None, :], 0), axis=1)
+    unpacked = jnp.take(incoming, slot_of, axis=0)
     kt = 2
     qt = per_device // kt
     block = unpacked.reshape(kt, qt, tile, tile).transpose(0, 2, 1, 3).reshape(kt, tile, qt * tile)

time: 178 us -> 179 us (level)
  matrix products: 11.6 us -> 9.45 us
  other arithmetic: 1.52 us -> 3.33 us
    gather x0 -> x2, local copies, waits for them, and re-layouts: none -> 2.62 us  [the longest x1 1.87 us: body(): unpacked = jnp.take(incoming, slot_of, axis=0)]
    dot_general x2 -> x0, matrix products: 2.52 us -> none  [the longest x1 1.92 us: body(): jnp.einsum('ps,sij->pij', unpack, incoming, preferred_element_type=jnp.fl...]
where the time goes in v17:
time: 179 us
  Pallas kernels  162 us (91%)
  matrix products  9.45 us (5%)
  local copies, waits for them, and re-layouts  4.76 us (3%)
  other arithmetic  3.33 us (2%)
    pallas_call x1, Pallas kernels, exchange(): pl.pallas_call(functools.partial(exchange_kernel, groups), out_shape=[jax...  83.3 us
    pallas_call x1, Pallas kernels, row_exchange(): pl.pallas_call(row_kernel, out_shape=[jax.ShapeDtypeStruct(a_out, a.dtype...  78.2 us
    dot_general x1, matrix products, body(): jnp.einsum('ckhypj,cyhkjn->pn', a, g, preferred_element_type=jnp.float32)  9.45 us

profile of v17, /device:TPU:89, one launch (start us, length us, event | category | flops | bytes accessed | tf_op | source)
XLA Modules:
  0.0 179.1 jit_solution(1011149866288590616)
XLA Ops:
  0.0 0.0 copy-start
  0.0 1.0 copy-done
  1.0 0.7 fusion.16
  1.7 0.1 select_reduce_fusion
  1.9 0.7 gather_fusion
  2.6 1.1 broadcast_select_fusion.refs_0_
  3.8 83.3 %exchange_z_lox_z_lo_z_lox.1 = (bf16[32,128,128]{2,1,0:T(8,128)(2,1)}, bf16[8,512,128]{2,1,0:T(8,128)(2,1)}, s32[32,1,16]{2,1,0:T(1,128)}) custom-call(bf16[32,128,128]{2,1,0:T(8,128)(2,1)} %broadcast_select_fusion.refs_0_, bf16[512,128]{1,0:T(8,128)(2,1)} %refs_1_.1, s32[1,16]{1,0:T(1,128)} %refs_2_.1), custom_call_target="tpu_custom_call" | custom-call | bytes 4198400 | tf_op jit(solution)/shard_map/exchange_z_lox_z_lo_z_lox/pallas_call | solution.py:148
  87.1 0.9 fusion.11
  87.9 0.2 select_reduce_fusion.1
  88.1 0.1 reduce_sum.37
  88.2 1.9 %gather_fusion.1 = bf16[16,128,128]{2,1,0:T(8,128)(2,1)S(1)} fusion(bf16[32,128,128]{2,1,0:T(8,128)(2,1)} %get-tuple-element.12, s32[1024]{0:T(1024)S(1)} %pad_clamp_fusion), kind=kCustom, calls=%fused_computation.1 | custom fusion | bytes 1048640 | tf_op jit(solution)/shard_map/jit(_take)/gather | solution.py:295
  90.1 0.3 fusion.7
  90.5 1.0 reshape.56.b_ref
  91.5 78.2 %row_exchange.1 = (bf16[4,8,512,128]{3,2,1,0:T(8,128)(2,1)}, bf16[2,4,2,2,128,1024]{5,4,3,2,1,0:T(8,128)(2,1)}) custom-call(bf16[8,512,128]{2,1,0:T(8,128)(2,1)} %get-tuple-element.10.a_ref, bf16[2,128,1024]{2,1,0:T(8,128)(2,1)} %reshape.56.b_ref), custom_call_target="tpu_custom_call" | custom-call | bytes 25165824 | tf_op jit(solution)/shard_map/row_exchange/pallas_call | solution.py:261
  169.7 9.4 %bitcast_add_fusion = f32[512,1024]{1,0:T(8,128)} fusion(f32[512,1024]{1,0:T(8,128)} %param.7, bf16[2,4,2,2,128,1024]{5,4,3,2,1,0:T(8,128)(2,1)} %get-tuple-element.14, bf16[2,2,2,4,512,128]{5,4,3,2,1,0:T(8,128)(2,1)} %bitcast.25), kind=kOutput, calls=%fused_computation.5 | convolution fusion | flops 4295491584 | bytes 16777216 | tf_op jit(solution)/shard_map/ckhypj,cyhkjn->pn/dot_general | solution.py:301
  (7 shorter events, 0.0 us)
Async XLA Ops:
  0.0 1.0 copy-start

commit v18 on v16

--- a/solution.py
+++ b/solution.py
@@ -207,12 +207,12 @@
             block = g_ref.at[c, yy, hh, half]
             send(block, block, c_send.at[yy, hh, half], c_recv.at[yy, hh, half], core)
 
-    send(a_ref, ao_ref.at[xi], xd_send.at[0], xd_recv.at[0], {"x": up_x})
-    send(a_ref, ao_ref.at[xi], xd_send.at[1], xd_recv.at[1], {"x": dn_x})
     rows = b_ref.shape[1] // 4
     pieces = [(kk, pl.ds(part * rows, rows)) for kk in range(2) for part in range(4)]
     for p, (kk, span) in enumerate(pieces):
         send(b_ref.at[kk, span], g_ref.at[c, y, h, kk, span], z_send.at[p], z_recv.at[p], zpeer)
+    send(a_ref, ao_ref.at[xi], xd_send.at[0], xd_recv.at[0], {"x": up_x})
+    send(a_ref, ao_ref.at[xi], xd_send.at[1], xd_recv.at[1], {"x": dn_x})
     send(b_ref, g_ref.at[c, y, h], yd_send.at[0, 0], yd_recv.at[0, 0], {"y": up_y})
     send(b_ref, g_ref.at[c, y, h], yd_send.at[1, 0], yd_recv.at[1, 0], {"y": dn_y})
     for half in range(2):

time: 178 us -> 178 us (level)
  no operation moved by 1% of the time
where the time goes in v18:
time: 178 us
  Pallas kernels  162 us (91%)
  matrix products  11.6 us (7%)
  local copies, waits for them, and re-layouts  3.48 us (2%)
    pallas_call x1, Pallas kernels, exchange(): pl.pallas_call(functools.partial(exchange_kernel, groups), out_shape=[jax...  83.3 us
    pallas_call x1, Pallas kernels, row_exchange(): pl.pallas_call(row_kernel, out_shape=[jax.ShapeDtypeStruct(a_out, a.dtype...  78.2 us
    dot_general x1, matrix products, body(): jnp.einsum('ckhypj,cyhkjn->pn', a, g, preferred_element_type=jnp.float32)  9.13 us

profile of v18, /device:TPU:89, one launch (start us, length us, event | category | flops | bytes accessed | tf_op | source)
XLA Modules:
  0.0 178.2 jit_solution(16827048640133961007)
XLA Ops:
  0.0 0.0 copy-start
  0.0 1.0 copy-done
  1.0 0.7 fusion.24
  1.7 0.6 fusion.9
  2.3 0.0 copy-start.1
  2.3 1.4 copy.26.refs_0_
  3.7 83.3 %exchange_z_lox_z_lo_z_lox.1 = (bf16[32,128,128]{2,1,0:T(8,128)(2,1)}, bf16[8,512,128]{2,1,0:T(8,128)(2,1)}, s32[32,1,16]{2,1,0:T(1,128)}) custom-call(bf16[32,128,128]{2,1,0:T(8,128)(2,1)} %copy.26.refs_0_, bf16[512,128]{1,0:T(8,128)(2,1)} %refs_1_.1, s32[1,16]{1,0:T(1,128)} %refs_2_.1), custom_call_target="tpu_custom_call" | custom-call | bytes 4198400 | tf_op jit(solution)/shard_map/exchange_z_lox_z_lo_z_lox/pallas_call | solution.py:148
  87.0 0.9 fusion.14
  87.9 1.9 %fusion.7 = bf16[2,8,128,128]{3,1,0,2:T(8,128)(2,1)S(1)} fusion(bf16[32,128,128]{2,1,0:T(8,128)(2,1)} %get-tuple-element.12, s32[32]{0:T(128)S(1)} %fusion.14, s32[16]{0:T(128)S(1)} %iota_add_fusion), kind=kOutput, calls=%fused_computation.6 | convolution fusion | flops 17039872 | bytes 1573056 | tf_op jit(solution)/shard_map/ps,sij->pij/dot_general | solution.py:294
  89.9 1.0 reshape.20.b_ref
  90.9 78.2 %row_exchange.1 = (bf16[4,8,512,128]{3,2,1,0:T(8,128)(2,1)}, bf16[2,4,2,2,128,1024]{5,4,3,2,1,0:T(8,128)(2,1)}) custom-call(bf16[8,512,128]{2,1,0:T(8,128)(2,1)} %get-tuple-element.10.a_ref, bf16[2,128,1024]{2,1,0:T(8,128)(2,1)} %reshape.20.b_ref), custom_call_target="tpu_custom_call" | custom-call | bytes 25165824 | tf_op jit(solution)/shard_map/row_exchange/pallas_call | solution.py:261
  169.1 0.0 copy-done.1
  169.1 9.1 %bitcast_add_fusion = f32[512,1024]{1,0:T(8,128)} fusion(f32[512,1024]{1,0:T(8,128)S(1)} %copy-done.1, bf16[2,4,2,2,128,1024]{5,4,3,2,1,0:T(8,128)(2,1)} %get-tuple-element.14, bf16[2,2,2,4,512,128]{5,4,3,2,1,0:T(8,128)(2,1)} %bitcast.25), kind=kOutput, calls=%fused_computation.3 | convolution fusion | flops 4295491584 | bytes 16777216 | tf_op jit(solution)/shard_map/ckhypj,cyhkjn->pn/dot_general | solution.py:302
  (2 shorter events, 0.0 us)
Async XLA Ops:
  0.0 1.0 copy-start
  2.3 166.7 %copy-start.1 = (f32[512,1024]{1,0:T(8,128)S(1)}, f32[512,1024]{1,0:T(8,128)}, u32[]{:S(2)}) copy-start(f32[512,1024]{1,0:T(8,128)} %param.7) | copy-start | bytes 6291460
